TPU v7x, 256 devices: a whole 4x4x8 slice. The times are simulated.
256 devices in a mesh: theta: 128 (over z, y_lo, x, core), gz: 2 (over y_hi).
Axes of the slice: x: 4, y: 4 (y_hi: 2, y_lo: 2; y = y_hi * 2 + y_lo), z: 8, core: 2. Of those that a mesh axis runs over, the one named last changes fastest.
Arguments:
- velocity: float32 [3, 2048, 16, 512], P(None, 'theta', 'gz'), may hold values from -2 to 3.5
- radial_op: float32 [512, 544], replicated, may hold values from -0.25 to 0.25
- azimuth_stencil: float32 [21], replicated, may hold values from -1.25 to 1.25
- viscous_factor: float32 [1], replicated, may hold values from 1000000 to 10000000
Outputs:
- new_velocity: float32 [3, 2048, 16, 512], P(None, 'theta', 'gz')
- nonlinear: float32 [3, 2048, 16, 512], P(None, 'theta', 'gz')
All inputs are finite; a program needn't handle non-finite values.
Results may differ from a plain program's by a relative error of at most 0.000098.
Values sent between devices are 32-bit elements; how exact they have to be, the bound alone decides.
A program may use at most 64 MiB of HBM per device.

v0:
```python
import jax
import jax.numpy as jnp
from jax import lax
from jax.sharding import PartitionSpec as P

AXIAL_WEIGHTS = (0.75, -0.15, 1.0 / 60.0)
STEP_WEIGHT = 0.2
MIRROR_SIGNS = (-1.0, -1.0, 1.0)


def partner_2(block, axis, bit):
    count = lax.axis_size(axis)
    route = []
    for low in range(count):
        high = low | 1 << bit
        if high != low and high < count:
            route += [(low, high), (high, low)]
    return lax.ppermute(block, axis, route)


def extended_2(shard, sides, width):
    for axis, dim in sides:
        peers, length = (lax.axis_size(axis), shard.shape[dim])
        up = [(i, (i + 1) % peers) for i in range(peers)]
        down = [(j, i) for i, j in up]
        last = lax.slice_in_dim(shard, length - width, length, axis=dim)
        initial = lax.slice_in_dim(shard, 0, width, axis=dim)
        before = lax.ppermute(last, axis, up)
        after = lax.ppermute(initial, axis, down)
        shard = jnp.concatenate([before, shard, after], axis=dim)
    return shard


def from_behind(shard, axis, by):
    peers = lax.axis_size(axis)
    return lax.ppermute(shard, axis, [(i, (i + by) % peers) for i in range(peers)])


def next_excess(excess):
    return 4.0 * excess * (1.0 - excess) / (1.0 + 4.0 * excess - 4.0 * excess * excess)


def reduce_step(center, lower_side, upper_side, excess):
    return (center - (excess - 0.5) * (lower_side + upper_side)) / (
        0.5 + 2.0 * excess - 2.0 * excess * excess
    )


def final_step(center, opposite, excess):
    return (center + (1.0 - 2.0 * excess) * opposite) / (4.0 * excess * (1.0 - excess))


def local(velocity, radial_op, azimuth_stencil, viscous_factor):
    cycle_size = lax.axis_size("theta")
    top_bit = cycle_size.bit_length() - 2
    points = velocity.shape[1]
    planes = velocity.shape[2]
    radial = velocity.shape[3]
    stencil_reach = (azimuth_stencil.shape[0] - 1) // 2
    tile_width = radial_op.shape[1] - radial
    highest = lax.Precision.HIGHEST
    radius = jnp.arange(radial).astype(jnp.float32) + 0.5
    inverse_r = 1.0 / radius
    sign_flip = jnp.array(MIRROR_SIGNS, jnp.float32).reshape(3, 1, 1, 1)
    partner = partner_2(velocity[:, :, :, :tile_width], "theta", top_bit)
    radial_grad = jnp.einsum("ctzj,ij->ctzi", velocity, radial_op[:, :radial], precision=highest)
    radial_grad = radial_grad + jnp.einsum(
        "ctzj,ij->ctzi", sign_flip * partner, radial_op[:, radial:], precision=highest
    )
    beside = extended_2(velocity, (("theta", 1),), stencil_reach)
    offset = (
        jnp.arange(points + 2 * stencil_reach, dtype=jnp.int32)[None, :]
        - jnp.arange(points, dtype=jnp.int32)[:, None]
    )
    selector = (
        offset[:, :, None] == jnp.arange(2 * stencil_reach + 1, dtype=jnp.int32)[None, None, :]
    ).astype(jnp.float32)
    band_matrix = jnp.einsum("pqk,k->pq", selector, azimuth_stencil, precision=highest)
    theta_grad = jnp.einsum("pq,cqzr->cpzr", band_matrix, beside, precision=highest)
    axial_ext = extended_2(velocity, (("gz", 2),), 3)
    axial_grad = jnp.zeros_like(velocity)
    for position, weight in enumerate(AXIAL_WEIGHTS):
        shift_by = position + 1
        upper_planes = axial_ext[:, :, 3 + shift_by : 3 + shift_by + planes]
        lower_planes = axial_ext[:, :, 3 - shift_by : 3 - shift_by + planes]
        axial_grad = axial_grad + weight * (upper_planes - lower_planes)
    radial_vel = velocity[0]
    azimuth_vel = velocity[1]
    axial_vel = velocity[2]
    convective = (
        radial_vel[None] * radial_grad
        + (azimuth_vel * inverse_r)[None] * theta_grad
        + axial_vel[None] * axial_grad
    )
    metric = jnp.stack(
        [
            -azimuth_vel * azimuth_vel * inverse_r,
            radial_vel * azimuth_vel * inverse_r,
            jnp.zeros_like(axial_vel),
        ]
    )
    nonlinear = convective + metric
    right_side = velocity - STEP_WEIGHT * nonlinear
    implicit_coef = viscous_factor[0] * inverse_r * inverse_r
    first_excess = 0.5 / (1.0 + 2.0 * implicit_coef)
    reduced = right_side * (2.0 * first_excess)
    excess = first_excess
    stride = 1
    while stride < points:
        extended = extended_2(reduced, (("theta", 1),), stride)
        reduced = reduce_step(reduced, extended[:, :points], extended[:, 2 * stride :], excess)
        excess = next_excess(excess)
        stride = stride * 2
    for bit_index in range(top_bit):
        hops = 1 << bit_index
        lower_side, upper_side = [
            from_behind(reduced, "theta", direction) for direction in (hops, cycle_size - hops)
        ]
        reduced = reduce_step(reduced, lower_side, upper_side, excess)
        excess = next_excess(excess)
    opposite = partner_2(reduced, "theta", top_bit)
    new_velocity = final_step(reduced, opposite, excess)
    return (new_velocity, nonlinear)


def solution(mesh):
    in_specs = (P(None, "theta", "gz", None), P(), P(), P())
    out_specs = (P(None, "theta", "gz", None), P(None, "theta", "gz", None))
    return jax.shard_map(local, mesh=mesh, in_specs=in_specs, out_specs=out_specs, check_vma=False)
```

profile of v0, /device:TPU:36, one launch (start us, length us, event | category | flops | bytes accessed | tf_op | source)
XLA Modules:
  0.0 314.6 jit_solution(5809262961963287841)
XLA Ops:
  3.9 3.3 %collective-permute-start.3 = (f32[3,16,3,512]{3,2,1,0:T(4,128)S(1)}, f32[3,16,3,512]{3,2,1,0:T(4,128)S(1)}, u32[]{:S(2)}, u32[]{:S(2)}) collective-permute-start(f32[3,16,3,512]{3,2,1,0:T(4,128)S(1)} %get-tuple-element.20), channel_id=1, source_target_pairs={{1,0},{0,1},{3,2},{2,3},{5,4},{4,5},{7,6},{6,7},{9,8},{8,9},{11,10... | collective-permute-start | bytes 884744 | tf_op jit(solution)/shard_map/ppermute | solution.py:29
  7.6 6.4 %collective-permute-start = (f32[3,16,8,32]{3,2,1,0:T(8,128)S(1)}, f32[3,16,8,32]{3,2,1,0:T(8,128)S(1)}, u32[]{:S(2)}, u32[]{:S(2)}) collective-permute-start(f32[3,16,8,32]{3,2,1,0:T(8,128)S(1)} %slice.112), channel_id=1, source_target_pairs={{0,128},{128,0},{2,130},{130,2},{4,132},{132,4},{6,134},{134,6},{8... | collective-permute-start | bytes 147464 | tf_op jit(solution)/shard_map/ppermute | solution.py:18
  24.6 2.8 subtract_multiply_fusion
  31.0 4.1 %collective-permute-done.6 = f32[3,1,8,512]{3,2,1,0:T(8,128)S(1)} collective-permute-done((f32[3,1,8,512]{3,2,1,0:T(8,128)S(1)}, f32[3,1,8,512]{3,2,1,0:T(8,128)S(1)}, u32[]{:S(2)}, u32[]{:S(2)}) %collective-permute-start.6) | collective-permute-done | bytes 49184 | tf_op jit(solution)/shard_map/ppermute | solution.py:29
  35.2 3.0 collective-permute-start.7
  50.0 5.2 %collective-permute-done.11 = f32[3,8,8,512]{3,2,1,0:T(8,128)S(1)} collective-permute-done((f32[3,8,8,512]{3,2,1,0:T(8,128)S(1)}, f32[3,8,8,512]{3,2,1,0:T(8,128)S(1)}, u32[]{:S(2)}, u32[]{:S(2)}) %collective-permute-start.11) | collective-permute-done | bytes 393248 | tf_op jit(solution)/shard_map/ppermute | solution.py:28
  55.5 6.6 %collective-permute-start.13 = (f32[3,16,8,512]{3,2,1,0:T(8,128)S(1)}, f32[3,16,8,512]{3,2,1,0:T(8,128)S(1)}, u32[]{:S(2)}, u32[]{:S(2)}) collective-permute-start(f32[3,16,8,512]{3,2,1,0:T(8,128)S(1)} %fusion.25), channel_id=1, source_target_pairs={{0,2},{2,4},{4,6},{6,8},{8,10},{10,12},{12,14},{14,16},{16,18},{18... | collective-permute-start | bytes 2359304 | tf_op jit(solution)/shard_map/ppermute | solution.py:36
  62.1 5.3 %collective-permute-done.13 = f32[3,16,8,512]{3,2,1,0:T(8,128)S(1)} collective-permute-done((f32[3,16,8,512]{3,2,1,0:T(8,128)S(1)}, f32[3,16,8,512]{3,2,1,0:T(8,128)S(1)}, u32[]{:S(2)}, u32[]{:S(2)}) %collective-permute-start.13) | collective-permute-done | bytes 786464 | tf_op jit(solution)/shard_map/ppermute | solution.py:36
  67.4 4.1 %collective-permute-done.14 = f32[3,16,8,512]{3,2,1,0:T(8,128)S(1)} collective-permute-done((f32[3,16,8,512]{3,2,1,0:T(8,128)S(1)}, f32[3,16,8,512]{3,2,1,0:T(8,128)S(1)}, u32[]{:S(2)}, u32[]{:S(2)}) %collective-permute-start.14) | collective-permute-done | bytes 786464 | tf_op jit(solution)/shard_map/ppermute | solution.py:36
  71.8 7.4 %collective-permute-start.15 = (f32[3,16,8,512]{3,2,1,0:T(8,128)S(1)}, f32[3,16,8,512]{3,2,1,0:T(8,128)S(1)}, u32[]{:S(2)}, u32[]{:S(2)}) collective-permute-start(f32[3,16,8,512]{3,2,1,0:T(8,128)S(1)} %subtract_divide_fusion.5), channel_id=1, source_target_pairs={{0,4},{2,6},{4,8},{6,10},{8,12},{10,14},{12,16},{14,18},{16,20},{1... | collective-permute-start | bytes 2359304 | tf_op jit(solution)/shard_map/ppermute | solution.py:36
  79.3 14.7 %collective-permute-done.15 = f32[3,16,8,512]{3,2,1,0:T(8,128)S(1)} collective-permute-done((f32[3,16,8,512]{3,2,1,0:T(8,128)S(1)}, f32[3,16,8,512]{3,2,1,0:T(8,128)S(1)}, u32[]{:S(2)}, u32[]{:S(2)}) %collective-permute-start.15) | collective-permute-done | bytes 786464 | tf_op jit(solution)/shard_map/ppermute | solution.py:36
  93.9 6.6 %collective-permute-done.16 = f32[3,16,8,512]{3,2,1,0:T(8,128)S(1)} collective-permute-done((f32[3,16,8,512]{3,2,1,0:T(8,128)S(1)}, f32[3,16,8,512]{3,2,1,0:T(8,128)S(1)}, u32[]{:S(2)}, u32[]{:S(2)}) %collective-permute-start.16) | collective-permute-done | bytes 786464 | tf_op jit(solution)/shard_map/ppermute | solution.py:36
  100.8 3.5 %collective-permute-start.17 = (f32[3,16,8,512]{3,2,1,0:T(8,128)S(1)}, f32[3,16,8,512]{3,2,1,0:T(8,128)S(1)}, u32[]{:S(2)}, u32[]{:S(2)}) collective-permute-start(f32[3,16,8,512]{3,2,1,0:T(8,128)S(1)} %subtract_divide_fusion.4), channel_id=1, source_target_pairs={{0,8},{2,10},{4,12},{6,14},{8,16},{10,18},{12,20},{14,22},{16,24},... | collective-permute-start | bytes 2359304 | tf_op jit(solution)/shard_map/ppermute | solution.py:36
  104.3 6.4 %collective-permute-start.18 = (f32[3,16,8,512]{3,2,1,0:T(8,128)S(1)}, f32[3,16,8,512]{3,2,1,0:T(8,128)S(1)}, u32[]{:S(2)}, u32[]{:S(2)}) collective-permute-start(f32[3,16,8,512]{3,2,1,0:T(8,128)S(1)} %subtract_divide_fusion.4), channel_id=1, source_target_pairs={{0,248},{2,250},{4,252},{6,254},{8,0},{10,2},{12,4},{14,6},{16,8},... | collective-permute-start | bytes 2359304 | tf_op jit(solution)/shard_map/ppermute | solution.py:36
  110.8 33.2 %collective-permute-done.17 = f32[3,16,8,512]{3,2,1,0:T(8,128)S(1)} collective-permute-done((f32[3,16,8,512]{3,2,1,0:T(8,128)S(1)}, f32[3,16,8,512]{3,2,1,0:T(8,128)S(1)}, u32[]{:S(2)}, u32[]{:S(2)}) %collective-permute-start.17) | collective-permute-done | bytes 786464 | tf_op jit(solution)/shard_map/ppermute | solution.py:36
  146.5 2.9 collective-permute-start.20
  149.5 31.0 %collective-permute-done.19 = f32[3,16,8,512]{3,2,1,0:T(8,128)S(1)} collective-permute-done((f32[3,16,8,512]{3,2,1,0:T(8,128)S(1)}, f32[3,16,8,512]{3,2,1,0:T(8,128)S(1)}, u32[]{:S(2)}, u32[]{:S(2)}) %collective-permute-start.19) | collective-permute-done | bytes 786464 | tf_op jit(solution)/shard_map/ppermute | solution.py:36
  180.5 3.1 collective-permute-done.20
  183.9 11.1 %collective-permute-start.21 = (f32[3,16,8,512]{3,2,1,0:T(8,128)S(1)}, f32[3,16,8,512]{3,2,1,0:T(8,128)S(1)}, u32[]{:S(2)}, u32[]{:S(2)}) collective-permute-start(f32[3,16,8,512]{3,2,1,0:T(8,128)S(1)} %subtract_divide_fusion.2), channel_id=1, source_target_pairs={{0,32},{2,34},{4,36},{6,38},{8,40},{10,42},{12,44},{14,46},{16,48}... | collective-permute-start | bytes 2359304 | tf_op jit(solution)/shard_map/ppermute | solution.py:36
  195.1 15.9 %collective-permute-done.21 = f32[3,16,8,512]{3,2,1,0:T(8,128)S(1)} collective-permute-done((f32[3,16,8,512]{3,2,1,0:T(8,128)S(1)}, f32[3,16,8,512]{3,2,1,0:T(8,128)S(1)}, u32[]{:S(2)}, u32[]{:S(2)}) %collective-permute-start.21) | collective-permute-done | bytes 786464 | tf_op jit(solution)/shard_map/ppermute | solution.py:36
  211.0 18.1 %collective-permute-done.22 = f32[3,16,8,512]{3,2,1,0:T(8,128)S(1)} collective-permute-done((f32[3,16,8,512]{3,2,1,0:T(8,128)S(1)}, f32[3,16,8,512]{3,2,1,0:T(8,128)S(1)}, u32[]{:S(2)}, u32[]{:S(2)}) %collective-permute-start.22) | collective-permute-done | bytes 786464 | tf_op jit(solution)/shard_map/ppermute | solution.py:36
  229.4 2.8 collective-permute-start.23
  233.7 39.4 %collective-permute-done.23 = f32[3,16,8,512]{3,2,1,0:T(8,128)S(1)} collective-permute-done((f32[3,16,8,512]{3,2,1,0:T(8,128)S(1)}, f32[3,16,8,512]{3,2,1,0:T(8,128)S(1)}, u32[]{:S(2)}, u32[]{:S(2)}) %collective-permute-start.23) | collective-permute-done | bytes 786464 | tf_op jit(solution)/shard_map/ppermute | solution.py:36
  273.6 40.0 %collective-permute-done.25 = f32[3,16,8,512]{3,2,1,0:T(8,128)S(1)} collective-permute-done((f32[3,16,8,512]{3,2,1,0:T(8,128)S(1)}, f32[3,16,8,512]{3,2,1,0:T(8,128)S(1)}, u32[]{:S(2)}, u32[]{:S(2)}) %collective-permute-start.25) | collective-permute-done | bytes 786464 | tf_op jit(solution)/shard_map/ppermute | solution.py:18
  (79 shorter events, 35.9 us)
Async XLA Ops:
  2.0 15.8 %collective-permute-start.1 = (f32[3,10,8,512]{3,2,1,0:T(8,128)S(1)}, f32[3,10,8,512]{3,2,1,0:T(8,128)S(1)}, u32[]{:S(2)}, u32[]{:S(2)}) collective-permute-start(f32[3,10,8,512]{3,2,1,0:T(8,128)S(1)} %get-tuple-element.18), channel_id=1, source_target_pairs={{0,2},{2,4},{4,6},{6,8},{8,10},{10,12},{12,14},{14,16},{16,18},{18... | collective-permute-start | bytes 1474568 | tf_op jit(solution)/shard_map/ppermute | solution.py:28
  2.1 16.0 %collective-permute-start.2 = (f32[3,10,8,512]{3,2,1,0:T(8,128)S(1)}, f32[3,10,8,512]{3,2,1,0:T(8,128)S(1)}, u32[]{:S(2)}, u32[]{:S(2)}) collective-permute-start(f32[3,10,8,512]{3,2,1,0:T(8,128)S(1)} %get-tuple-element.19), channel_id=1, source_target_pairs={{2,0},{4,2},{6,4},{8,6},{10,8},{12,10},{14,12},{16,14},{18,16},{20... | collective-permute-start | bytes 1474568 | tf_op jit(solution)/shard_map/ppermute | solution.py:29
  3.9 13.7 %collective-permute-start.3 = (f32[3,16,3,512]{3,2,1,0:T(4,128)S(1)}, f32[3,16,3,512]{3,2,1,0:T(4,128)S(1)}, u32[]{:S(2)}, u32[]{:S(2)}) collective-permute-start(f32[3,16,3,512]{3,2,1,0:T(4,128)S(1)} %get-tuple-element.20), channel_id=1, source_target_pairs={{1,0},{0,1},{3,2},{2,3},{5,4},{4,5},{7,6},{6,7},{9,8},{8,9},{11,10... | collective-permute-start | bytes 884744 | tf_op jit(solution)/shard_map/ppermute | solution.py:29
  7.2 17.3 %collective-permute-start.4 = (f32[3,16,3,512]{3,2,1,0:T(4,128)S(1)}, f32[3,16,3,512]{3,2,1,0:T(4,128)S(1)}, u32[]{:S(2)}, u32[]{:S(2)}) collective-permute-start(f32[3,16,3,512]{3,2,1,0:T(4,128)S(1)} %get-tuple-element.21), channel_id=1, source_target_pairs={{0,1},{1,0},{2,3},{3,2},{4,5},{5,4},{6,7},{7,6},{8,9},{9,8},{10,11... | collective-permute-start | bytes 884744 | tf_op jit(solution)/shard_map/ppermute | solution.py:28
  7.6 14.8 %collective-permute-start = (f32[3,16,8,32]{3,2,1,0:T(8,128)S(1)}, f32[3,16,8,32]{3,2,1,0:T(8,128)S(1)}, u32[]{:S(2)}, u32[]{:S(2)}) collective-permute-start(f32[3,16,8,32]{3,2,1,0:T(8,128)S(1)} %slice.112), channel_id=1, source_target_pairs={{0,128},{128,0},{2,130},{130,2},{4,132},{132,4},{6,134},{134,6},{8... | collective-permute-start | bytes 147464 | tf_op jit(solution)/shard_map/ppermute | solution.py:18
  27.5 7.6 %collective-permute-start.6 = (f32[3,1,8,512]{3,2,1,0:T(8,128)S(1)}, f32[3,1,8,512]{3,2,1,0:T(8,128)S(1)}, u32[]{:S(2)}, u32[]{:S(2)}) collective-permute-start(f32[3,1,8,512]{3,2,1,0:T(8,128)S(1)} %get-tuple-element.12), channel_id=1, source_target_pairs={{2,0},{4,2},{6,4},{8,6},{10,8},{12,10},{14,12},{16,14},{18,16},{20... | collective-permute-start | bytes 147464 | tf_op jit(solution)/shard_map/ppermute | solution.py:29
  35.2 4.3 %collective-permute-start.7 = (f32[3,2,8,512]{3,2,1,0:T(8,128)S(1)}, f32[3,2,8,512]{3,2,1,0:T(8,128)S(1)}, u32[]{:S(2)}, u32[]{:S(2)}) collective-permute-start(f32[3,2,8,512]{3,2,1,0:T(8,128)S(1)} %get-tuple-element.9), channel_id=1, source_target_pairs={{0,2},{2,4},{4,6},{6,8},{8,10},{10,12},{12,14},{14,16},{16,18},{18... | collective-permute-start | bytes 294920 | tf_op jit(solution)/shard_map/ppermute | solution.py:28
  40.7 5.1 %collective-permute-start.10 = (f32[3,4,8,512]{3,2,1,0:T(8,128)S(1)}, f32[3,4,8,512]{3,2,1,0:T(8,128)S(1)}, u32[]{:S(2)}, u32[]{:S(2)}) collective-permute-start(f32[3,4,8,512]{3,2,1,0:T(8,128)S(1)} %get-tuple-element.8), channel_id=1, source_target_pairs={{2,0},{4,2},{6,4},{8,6},{10,8},{12,10},{14,12},{16,14},{18,16},{20... | collective-permute-start | bytes 589832 | tf_op jit(solution)/shard_map/ppermute | solution.py:29
  42.6 5.1 %collective-permute-start.9 = (f32[3,4,8,512]{3,2,1,0:T(8,128)S(1)}, f32[3,4,8,512]{3,2,1,0:T(8,128)S(1)}, u32[]{:S(2)}, u32[]{:S(2)}) collective-permute-start(f32[3,4,8,512]{3,2,1,0:T(8,128)S(1)} %get-tuple-element.7), channel_id=1, source_target_pairs={{0,2},{2,4},{4,6},{6,8},{8,10},{10,12},{12,14},{14,16},{16,18},{18... | collective-permute-start | bytes 589832 | tf_op jit(solution)/shard_map/ppermute | solution.py:28
  47.9 7.3 %collective-permute-start.11 = (f32[3,8,8,512]{3,2,1,0:T(8,128)S(1)}, f32[3,8,8,512]{3,2,1,0:T(8,128)S(1)}, u32[]{:S(2)}, u32[]{:S(2)}) collective-permute-start(f32[3,8,8,512]{3,2,1,0:T(8,128)S(1)} %get-tuple-element.5), channel_id=1, source_target_pairs={{0,2},{2,4},{4,6},{6,8},{8,10},{10,12},{12,14},{14,16},{16,18},{18... | collective-permute-start | bytes 1179656 | tf_op jit(solution)/shard_map/ppermute | solution.py:28
  50.0 5.3 %collective-permute-start.12 = (f32[3,8,8,512]{3,2,1,0:T(8,128)S(1)}, f32[3,8,8,512]{3,2,1,0:T(8,128)S(1)}, u32[]{:S(2)}, u32[]{:S(2)}) collective-permute-start(f32[3,8,8,512]{3,2,1,0:T(8,128)S(1)} %get-tuple-element.6), channel_id=1, source_target_pairs={{2,0},{4,2},{6,4},{8,6},{10,8},{12,10},{14,12},{16,14},{18,16},{20... | collective-permute-start | bytes 1179656 | tf_op jit(solution)/shard_map/ppermute | solution.py:29
  55.5 12.0 %collective-permute-start.13 = (f32[3,16,8,512]{3,2,1,0:T(8,128)S(1)}, f32[3,16,8,512]{3,2,1,0:T(8,128)S(1)}, u32[]{:S(2)}, u32[]{:S(2)}) collective-permute-start(f32[3,16,8,512]{3,2,1,0:T(8,128)S(1)} %fusion.25), channel_id=1, source_target_pairs={{0,2},{2,4},{4,6},{6,8},{8,10},{10,12},{12,14},{14,16},{16,18},{18... | collective-permute-start | bytes 2359304 | tf_op jit(solution)/shard_map/ppermute | solution.py:36
  62.0 9.5 %collective-permute-start.14 = (f32[3,16,8,512]{3,2,1,0:T(8,128)S(1)}, f32[3,16,8,512]{3,2,1,0:T(8,128)S(1)}, u32[]{:S(2)}, u32[]{:S(2)}) collective-permute-start(f32[3,16,8,512]{3,2,1,0:T(8,128)S(1)} %fusion.25), channel_id=1, source_target_pairs={{0,254},{2,0},{4,2},{6,4},{8,6},{10,8},{12,10},{14,12},{16,14},{18... | collective-permute-start | bytes 2359304 | tf_op jit(solution)/shard_map/ppermute | solution.py:36
  71.8 22.1 %collective-permute-start.15 = (f32[3,16,8,512]{3,2,1,0:T(8,128)S(1)}, f32[3,16,8,512]{3,2,1,0:T(8,128)S(1)}, u32[]{:S(2)}, u32[]{:S(2)}) collective-permute-start(f32[3,16,8,512]{3,2,1,0:T(8,128)S(1)} %subtract_divide_fusion.5), channel_id=1, source_target_pairs={{0,4},{2,6},{4,8},{6,10},{8,12},{10,14},{12,16},{14,18},{16,20},{1... | collective-permute-start | bytes 2359304 | tf_op jit(solution)/shard_map/ppermute | solution.py:36
  79.2 21.3 %collective-permute-start.16 = (f32[3,16,8,512]{3,2,1,0:T(8,128)S(1)}, f32[3,16,8,512]{3,2,1,0:T(8,128)S(1)}, u32[]{:S(2)}, u32[]{:S(2)}) collective-permute-start(f32[3,16,8,512]{3,2,1,0:T(8,128)S(1)} %subtract_divide_fusion.5), channel_id=1, source_target_pairs={{0,252},{2,254},{4,0},{6,2},{8,4},{10,6},{12,8},{14,10},{16,12},{1... | collective-permute-start | bytes 2359304 | tf_op jit(solution)/shard_map/ppermute | solution.py:36
  100.8 43.2 %collective-permute-start.17 = (f32[3,16,8,512]{3,2,1,0:T(8,128)S(1)}, f32[3,16,8,512]{3,2,1,0:T(8,128)S(1)}, u32[]{:S(2)}, u32[]{:S(2)}) collective-permute-start(f32[3,16,8,512]{3,2,1,0:T(8,128)S(1)} %subtract_divide_fusion.4), channel_id=1, source_target_pairs={{0,8},{2,10},{4,12},{6,14},{8,16},{10,18},{12,20},{14,22},{16,24},... | collective-permute-start | bytes 2359304 | tf_op jit(solution)/shard_map/ppermute | solution.py:36
  104.3 41.8 %collective-permute-start.18 = (f32[3,16,8,512]{3,2,1,0:T(8,128)S(1)}, f32[3,16,8,512]{3,2,1,0:T(8,128)S(1)}, u32[]{:S(2)}, u32[]{:S(2)}) collective-permute-start(f32[3,16,8,512]{3,2,1,0:T(8,128)S(1)} %subtract_divide_fusion.4), channel_id=1, source_target_pairs={{0,248},{2,250},{4,252},{6,254},{8,0},{10,2},{12,4},{14,6},{16,8},... | collective-permute-start | bytes 2359304 | tf_op jit(solution)/shard_map/ppermute | solution.py:36
  146.4 34.1 %collective-permute-start.19 = (f32[3,16,8,512]{3,2,1,0:T(8,128)S(1)}, f32[3,16,8,512]{3,2,1,0:T(8,128)S(1)}, u32[]{:S(2)}, u32[]{:S(2)}) collective-permute-start(f32[3,16,8,512]{3,2,1,0:T(8,128)S(1)} %subtract_divide_fusion.3), channel_id=1, source_target_pairs={{0,16},{2,18},{4,20},{6,22},{8,24},{10,26},{12,28},{14,30},{16,32}... | collective-permute-start | bytes 2359304 | tf_op jit(solution)/shard_map/ppermute | solution.py:36
  146.5 37.1 %collective-permute-start.20 = (f32[3,16,8,512]{3,2,1,0:T(8,128)S(1)}, f32[3,16,8,512]{3,2,1,0:T(8,128)S(1)}, u32[]{:S(2)}, u32[]{:S(2)}) collective-permute-start(f32[3,16,8,512]{3,2,1,0:T(8,128)S(1)} %subtract_divide_fusion.3), channel_id=1, source_target_pairs={{0,240},{2,242},{4,244},{6,246},{8,248},{10,250},{12,252},{14,254}... | collective-permute-start | bytes 2359304 | tf_op jit(solution)/shard_map/ppermute | solution.py:36
  183.9 27.2 %collective-permute-start.21 = (f32[3,16,8,512]{3,2,1,0:T(8,128)S(1)}, f32[3,16,8,512]{3,2,1,0:T(8,128)S(1)}, u32[]{:S(2)}, u32[]{:S(2)}) collective-permute-start(f32[3,16,8,512]{3,2,1,0:T(8,128)S(1)} %subtract_divide_fusion.2), channel_id=1, source_target_pairs={{0,32},{2,34},{4,36},{6,38},{8,40},{10,42},{12,44},{14,46},{16,48}... | collective-permute-start | bytes 2359304 | tf_op jit(solution)/shard_map/ppermute | solution.py:36
  195.0 34.1 %collective-permute-start.22 = (f32[3,16,8,512]{3,2,1,0:T(8,128)S(1)}, f32[3,16,8,512]{3,2,1,0:T(8,128)S(1)}, u32[]{:S(2)}, u32[]{:S(2)}) collective-permute-start(f32[3,16,8,512]{3,2,1,0:T(8,128)S(1)} %subtract_divide_fusion.2), channel_id=1, source_target_pairs={{0,224},{2,226},{4,228},{6,230},{8,232},{10,234},{12,236},{14,238}... | collective-permute-start | bytes 2359304 | tf_op jit(solution)/shard_map/ppermute | solution.py:36
  229.4 43.7 %collective-permute-start.23 = (f32[3,16,8,512]{3,2,1,0:T(8,128)S(1)}, f32[3,16,8,512]{3,2,1,0:T(8,128)S(1)}, u32[]{:S(2)}, u32[]{:S(2)}) collective-permute-start(f32[3,16,8,512]{3,2,1,0:T(8,128)S(1)} %subtract_divide_fusion.1), channel_id=1, source_target_pairs={{0,64},{2,66},{4,68},{6,70},{8,72},{10,74},{12,76},{14,78},{16,80}... | collective-permute-start | bytes 2359304 | tf_op jit(solution)/shard_map/ppermute | solution.py:36
  232.2 40.9 %collective-permute-start.24 = (f32[3,16,8,512]{3,2,1,0:T(8,128)S(1)}, f32[3,16,8,512]{3,2,1,0:T(8,128)S(1)}, u32[]{:S(2)}, u32[]{:S(2)}) collective-permute-start(f32[3,16,8,512]{3,2,1,0:T(8,128)S(1)} %subtract_divide_fusion.1), channel_id=1, source_target_pairs={{0,192},{2,194},{4,196},{6,198},{8,200},{10,202},{12,204},{14,206}... | collective-permute-start | bytes 2359304 | tf_op jit(solution)/shard_map/ppermute | solution.py:36
  273.4 40.2 %collective-permute-start.25 = (f32[3,16,8,512]{3,2,1,0:T(8,128)S(1)}, f32[3,16,8,512]{3,2,1,0:T(8,128)S(1)}, u32[]{:S(2)}, u32[]{:S(2)}) collective-permute-start(f32[3,16,8,512]{3,2,1,0:T(8,128)S(1)} %subtract_divide_fusion), channel_id=1, source_target_pairs={{0,128},{128,0},{2,130},{130,2},{4,132},{132,4},{6,134},{134,6},{8... | collective-permute-start | bytes 2359304 | tf_op jit(solution)/shard_map/ppermute | solution.py:18
  (6 other events, 30.8 us)
where the time goes:
time: 315 us
  waiting for transfers between devices  234 us (74%)
  starting transfers between devices  65 us (21%)
  matrix products  6.85 us (2%)
  other arithmetic  4.01 us (1%)
    ppermute x12, waiting for transfers between devices, from_behind(): lax.ppermute(shard, axis, [(i, (i + by) % peers) for i in range(peers)])  174 us
    ppermute x12, starting transfers between devices, from_behind(): lax.ppermute(shard, axis, [(i, (i + by) % peers) for i in range(peers)])  42.3 us
    ppermute x2, waiting for transfers between devices, partner_2(): return lax.ppermute(block, axis, route)  42 us
    ppermute x6, waiting for transfers between devices, extended_2(): before = lax.ppermute(last, axis, up)  12.3 us
    ppermute x6, starting transfers between devices, extended_2(): after = lax.ppermute(initial, axis, down)  8.66 us
    ppermute x6, starting transfers between devices, extended_2(): before = lax.ppermute(last, axis, up)  7.66 us
    ppermute x2, starting transfers between devices, partner_2(): return lax.ppermute(block, axis, route)  6.47 us
  transfers between devices with their start and end apart: 26, of which 22 were waited for; matrix products, arithmetic and copies ran while one was open for 2% of the time, Pallas kernels for 0%

commit v1 on v0

v1 whole, which is shorter than its diff:
```python
import functools

import jax
import jax.numpy as jnp
from jax import lax
from jax.experimental import pallas as pl
from jax.experimental.pallas import tpu as pltpu
from jax.sharding import PartitionSpec as P

AXIAL_WEIGHTS = (0.75, -0.15, 1.0 / 60.0)
STEP_WEIGHT = 0.2
MIRROR_SIGNS = (-1.0, -1.0, 1.0)
MESH = pl.DeviceIdType.MESH
F32 = jnp.float32
BF16 = jnp.bfloat16
REACH = 10
PTS = 16
NR = 512
RT = 32
LANES = 128
TILES = NR // LANES
GROUP = 8
SECTORS = 128
BLOCKS = SECTORS // GROUP
NT_DOT = (((1,), (1,)), ((), ()))


def split(x):
    high = x.astype(BF16)
    return high, (x - high.astype(F32)).astype(BF16)


def dot3(x, w_high, w_low):
    high, low = split(x)
    out = lax.dot_general(high, w_low, NT_DOT, preferred_element_type=F32)
    out = out + lax.dot_general(low, w_high, NT_DOT, preferred_element_type=F32)
    return out + lax.dot_general(high, w_high, NT_DOT, preferred_element_type=F32)


def sublane(shape):
    return lax.broadcasted_iota(jnp.int32, shape, len(shape) - 2)


def lane(shape):
    return lax.broadcasted_iota(jnp.int32, shape, len(shape) - 1)


def doubled(q):
    return q * (2.0 - q)


def kernel(
    v_hbm, op_hbm, sten, visc, new_hbm, non_hbm,
    ext, op_v, wh, wl, gsend, grecv, msend, mrecv, part, rhs, loc,
    rho_t, inv_t, pw_t, w_t, big_t, inv_n, fb, up_in, tot, car,
    in_sem, halo_s, halo_r, gz_s, gz_r, mir_s, mir_r, p1_s, p1_r, p2_s, p2_r, p3_s, p3_r, out_sem,
):
    p = lax.axis_index("theta")
    g = lax.axis_index("gz")
    me = p % GROUP
    block = p // GROUP
    backward = me // TILES
    my_tile = me % TILES

    reads = [
        pltpu.make_async_copy(v_hbm.at[c], ext.at[c, pl.ds(REACH, PTS)], in_sem.at[c]) for c in range(3)
    ]
    reads.append(pltpu.make_async_copy(op_hbm, op_v, in_sem.at[3]))
    for r in reads:
        r.start()

    after = (p + 1) % SECTORS
    before = (p + SECTORS - 1) % SECTORS
    across = (p + SECTORS // 2) % SECTORS
    group_peers = [block * GROUP + (me + k) % GROUP for k in range(1, GROUP)]
    block_peers = [((block + k) % BLOCKS) * GROUP + me for k in range(1, BLOCKS)]
    barrier = pltpu.get_barrier_semaphore()
    greeted = [(p, 1 - g), (after, g), (before, g)]
    greeted += [(q, g) for q in group_peers + block_peers]
    for who in greeted:
        pl.semaphore_signal(barrier, inc=1, device_id=who, device_id_type=MESH)

    for c in range(3):
        reads[c].wait()

    sub = sublane((8, NR))
    middle = (sub == 3) | (sub == 4)

    def pack(i, carry):
        for c in range(3):
            x = [ext[c, REACH + 4 * i + j] for j in range(4)]
            gsend[c, 3 * i] = jnp.where(middle, pltpu.roll(x[3], 3, 0), x[0])
            gsend[c, 3 * i + 1] = jnp.where(
                sub == 3, pltpu.roll(x[3], 1, 0), jnp.where(sub == 4, pltpu.roll(x[3], 7, 0), x[1])
            )
            gsend[c, 3 * i + 2] = jnp.where(middle, pltpu.roll(x[3], 5, 0), x[2])
            quarter = lane((8, LANES)) // RT
            line = x[0][:, :LANES]
            for j in range(1, 4):
                line = jnp.where(quarter == j, pltpu.roll(x[j][:, :LANES], RT * j, 1), line)
            msend[c, i] = MIRROR_SIGNS[c] * line
        return carry

    lax.fori_loop(0, 4, pack, 0)

    pl.semaphore_wait(barrier, len(greeted))

    def remote(src, dst, s_sem, r_sem, who):
        return pltpu.make_async_remote_copy(
            src_ref=src, dst_ref=dst, send_sem=s_sem, recv_sem=r_sem, device_id=who, device_id_type=MESH
        )

    halos, planes, mirrors = [], [], []
    for c in range(3):
        planes.append(remote(gsend.at[c], grecv.at[c], gz_s.at[c], gz_r.at[c], (p, 1 - g)))
        halos.append(
            (
                remote(
                    ext.at[c, pl.ds(PTS, REACH)], ext.at[c, pl.ds(0, REACH)],
                    halo_s.at[c, 0], halo_r.at[c, 0], (after, g),
                ),
                remote(
                    ext.at[c, pl.ds(REACH, REACH)], ext.at[c, pl.ds(REACH + PTS, REACH)],
                    halo_s.at[c, 1], halo_r.at[c, 1], (before, g),
                ),
            )
        )
        mirrors.append(remote(msend.at[c], mrecv.at[c], mir_s.at[c], mir_r.at[c], (across, g)))
        mirrors[c].start()
        halos[c][0].start()
        halos[c][1].start()
        planes[c].start()

    radius = lane((8, NR)).astype(F32) + 0.5
    inverse_r = 1.0 / radius
    inv_t[...] = inverse_r
    coef = visc[0] * inverse_r * inverse_r
    half = 0.5 / coef
    gap = jnp.sqrt(half * (2.0 + half)) - half
    rho = 1.0 - gap
    rho_t[...] = rho
    scale = 1.0 / jnp.sqrt(1.0 + 4.0 * coef)
    power = scale
    for j in range(PTS):
        power = power * rho
        pw_t[j] = power
    gap16 = doubled(doubled(doubled(doubled(gap))))
    gap128 = doubled(doubled(doubled(gap16)))
    whole = doubled(doubled(doubled(doubled(gap128))))
    for t in range(TILES):
        cols = slice(t * LANES, (t + 1) * LANES)
        w_t[t] = 1.0 - gap16[:, cols]
        big_t[t] = 1.0 - gap128[:, cols]
        inv_n[t] = 1.0 / whole[:, cols]

    reads[3].wait()
    op_high, op_low = split(op_v[...])
    wh[...] = op_high
    wl[...] = op_low
    for c in range(3):
        lines = ext[c, pl.ds(REACH, PTS)].reshape(PTS * 8, NR)
        part[c] = dot3(lines, wh[:, :NR], wl[:, :NR]).reshape(PTS, 8, NR)

    def first_half(c):
        mirrors[c].wait_recv()

        def unpack(i, carry):
            packed = mrecv[c, i]
            lines = [packed[:, :RT]] + [pltpu.roll(packed, LANES - RT * j, 1)[:, :RT] for j in range(1, 4)]
            lines = jnp.concatenate(lines, axis=0)
            more = dot3(lines, wh[:, NR:], wl[:, NR:]).reshape(4, 8, NR)
            rows = pl.ds(4 * i, 4)
            part[c, rows] = part[c, rows] + more
            return carry

        lax.fori_loop(0, 4, unpack, 0)
        halos[c][0].wait_recv()
        halos[c][1].wait_recv()

        def azimuth(i, carry):
            inv = inv_t[...]
            for t in range(4):
                row = 4 * i + t
                grad = sten[0] * ext[c, row]
                for m in range(1, 2 * REACH + 1):
                    grad = grad + sten[m] * ext[c, row + m]
                a, b = ext[0, REACH + row], ext[1, REACH + row]
                turn = b * inv
                term = a * part[c, row] + turn * grad
                if c == 0:
                    term = term - b * turn
                if c == 1:
                    term = term + a * turn
                part[c, row] = term
            return carry

        lax.fori_loop(0, 4, azimuth, 0)

    def second_half(c):
        planes[c].wait_recv()

        def axial(i, left):
            packed = [grecv[c, 3 * i + j] for j in range(3)]
            other = packed + [
                jnp.where(
                    sub < 2,
                    pltpu.roll(packed[0], 5, 0),
                    jnp.where(
                        sub == 2,
                        pltpu.roll(packed[1], 7, 0),
                        jnp.where(sub == 5, pltpu.roll(packed[1], 1, 0), pltpu.roll(packed[2], 3, 0)),
                    ),
                )
            ]
            rho = rho_t[...]
            for t in range(4):
                row = 4 * i + t
                own, far = ext[c, REACH + row], other[t]
                grad = jnp.zeros_like(own)
                for m, weight in enumerate(AXIAL_WEIGHTS, 1):
                    upper = pltpu.roll(jnp.where(sub < m, far, own), 8 - m, 0)
                    lower = pltpu.roll(jnp.where(sub >= 8 - m, far, own), m, 0)
                    grad = grad + weight * (upper - lower)
                term = part[c, row] + ext[2, REACH + row] * grad
                part[c, row] = term
                right = own - STEP_WEIGHT * term
                rhs[c, row] = right
                left = right + rho * left
                loc[c, row] = left - right
            return left

        left = lax.fori_loop(0, 4, axial, jnp.zeros((8, NR), F32))

        def back(i, carry):
            rho = rho_t[...]
            for t in range(4):
                row = PTS - 1 - 4 * i - t
                carry = rhs[c, row] + rho * carry
                loc[c, row] = loc[c, row] + carry
            return carry

        back_sum = lax.fori_loop(0, 4, back, jnp.zeros((8, NR), F32))
        for t in range(TILES):
            cols = slice(t * LANES, (t + 1) * LANES)
            fb[c, t] = left[:, cols]
            fb[c, TILES + t] = back_sum[:, cols]

    def start_group(c):
        copies = []
        for k in range(1, GROUP):
            other = (me + k) % GROUP
            cp = remote(
                fb.at[c, other], up_in.at[c, me], p1_s.at[c, k - 1], p1_r.at[c, k - 1],
                (block * GROUP + other, g),
            )
            cp.start()
            copies.append(cp)
        up_in[c, me] = fb[c, me]
        return copies

    def entry(c, k):
        return up_in[c, k + backward * (GROUP - 1 - 2 * k)]

    def start_blocks(c, arrivals):
        for cp in arrivals:
            cp.wait_recv()
        w = w_t[my_tile]
        run = entry(c, 0)
        for k in range(1, GROUP):
            run = entry(c, k) + w * run
        tot[c, block] = run
        copies = []
        for k in range(1, BLOCKS):
            cp = remote(
                tot.at[c, block], tot.at[c, block], p2_s.at[c, k - 1], p2_r.at[c, k - 1],
                (((block + k) % BLOCKS) * GROUP + me, g),
            )
            cp.start()
            copies.append(cp)
        return copies

    def start_return(c, arrivals):
        for cp in arrivals:
            cp.wait_recv()
        big = big_t[my_tile]
        run = tot[c, block]
        for m in range(BLOCKS - 1, 0, -1):
            run = tot[c, (block + (2 * backward - 1) * m + BLOCKS) % BLOCKS] + big * run
        run = run * inv_n[my_tile]
        w = w_t[my_tile]
        out = up_in
        for k in range(GROUP):
            here = k + backward * (GROUP - 1 - 2 * k)
            value = up_in[c, here]
            out[c, here] = run
            run = value + w * run
        copies = []
        for k in range(1, GROUP):
            other = (me + k) % GROUP
            cp = remote(
                up_in.at[c, other], car.at[c, me], p3_s.at[c, k - 1], p3_r.at[c, k - 1],
                (block * GROUP + other, g),
            )
            cp.start()
            copies.append(cp)
        car[c, me] = up_in[c, me]
        return copies

    def finish(c, arrivals):
        for cp in arrivals:
            cp.wait_recv()
        scale = 1.0 / jnp.sqrt(1.0 + 4.0 * (visc[0] * inv_t[...] * inv_t[...]))
        from_left = jnp.concatenate([car[c, t] for t in range(TILES)], axis=1)
        from_right = jnp.concatenate([car[c, TILES + t] for t in range(TILES)], axis=1)

        def last(i, carry):
            for t in range(4):
                row = 4 * i + t
                loc[c, row] = (
                    scale * loc[c, row] + pw_t[row] * from_left + pw_t[PTS - 1 - row] * from_right
                )
            return carry

        lax.fori_loop(0, 4, last, 0)

    def write(c, src, dst, k):
        cp = pltpu.make_async_copy(src.at[c], dst.at[c], out_sem.at[k, c])
        cp.start()
        return cp

    writes = []
    first_half(0)
    second_half(0)
    one = [start_group(0), None, None]
    writes.append(write(0, part, non_hbm, 1))
    first_half(1)
    second_half(1)
    one[1] = start_group(1)
    two = [start_blocks(0, one[0]), None, None]
    writes.append(write(1, part, non_hbm, 1))
    first_half(2)
    second_half(2)
    one[2] = start_group(2)
    two[1] = start_blocks(1, one[1])
    three = [start_return(0, two[0]), None, None]
    writes.append(write(2, part, non_hbm, 1))
    two[2] = start_blocks(2, one[2])
    three[1] = start_return(1, two[1])
    finish(0, three[0])
    writes.append(write(0, loc, new_hbm, 0))
    three[2] = start_return(2, two[2])
    finish(1, three[1])
    writes.append(write(1, loc, new_hbm, 0))
    finish(2, three[2])
    writes.append(write(2, loc, new_hbm, 0))
    for c in range(3):
        for cp in (planes[c], mirrors[c], *halos[c], *one[c], *two[c], *three[c]):
            cp.wait_send()
    for cp in writes:
        cp.wait()


def local(velocity, radial_op, azimuth_stencil, viscous_factor):
    dma = pltpu.SemaphoreType.DMA
    block = velocity.shape
    any_space = pl.BlockSpec(memory_space=pl.ANY)
    scalars = pl.BlockSpec(memory_space=pltpu.SMEM)
    tile = (8, LANES)
    return pl.pallas_call(
        kernel,
        name="substep",
        out_shape=(jax.ShapeDtypeStruct(block, F32), jax.ShapeDtypeStruct(block, F32)),
        in_specs=[any_space, any_space, scalars, scalars],
        out_specs=(any_space, any_space),
        scratch_shapes=[
            pltpu.VMEM((3, PTS + 2 * REACH, 8, NR), F32),
            pltpu.VMEM((NR, NR + RT), F32),
            pltpu.VMEM((NR, NR + RT), BF16),
            pltpu.VMEM((NR, NR + RT), BF16),
            pltpu.VMEM((3, 12, 8, NR), F32),
            pltpu.VMEM((3, 12, 8, NR), F32),
            pltpu.VMEM((3, 4, *tile), F32),
            pltpu.VMEM((3, 4, *tile), F32),
            pltpu.VMEM(block, F32),
            pltpu.VMEM(block, F32),
            pltpu.VMEM(block, F32),
            pltpu.VMEM((8, NR), F32),
            pltpu.VMEM((8, NR), F32),
            pltpu.VMEM((PTS, 8, NR), F32),
            pltpu.VMEM((TILES, *tile), F32),
            pltpu.VMEM((TILES, *tile), F32),
            pltpu.VMEM((TILES, *tile), F32),
            pltpu.VMEM((3, GROUP, *tile), F32),
            pltpu.VMEM((3, GROUP, *tile), F32),
            pltpu.VMEM((3, BLOCKS, *tile), F32),
            pltpu.VMEM((3, GROUP, *tile), F32),
            dma((4,)),
            dma((3, 2)), dma((3, 2)),
            dma((3,)), dma((3,)),
            dma((3,)), dma((3,)),
            dma((3, GROUP - 1)), dma((3, GROUP - 1)),
            dma((3, BLOCKS - 1)), dma((3, BLOCKS - 1)),
            dma((3, GROUP - 1)), dma((3, GROUP - 1)),
            dma((2, 3)),
        ],
        compiler_params=pltpu.CompilerParams(
            collective_id=0, has_side_effects=True, vmem_limit_bytes=40 << 20
        ),
    )(velocity, radial_op, azimuth_stencil, viscous_factor)


def solution(mesh):
    spec = P(None, "theta", "gz", None)
    return jax.shard_map(
        local, mesh=mesh, in_specs=(spec, P(), P(), P()), out_specs=(spec, spec), check_vma=False
    )
```

time: 315 us -> 51.9 us (0.16)
  the two profiles are of different devices: /device:TPU:36 before, /device:TPU:1 now
where the time goes in v1:
time: 51.9 us; the launch traced here: 51.7 us
  Pallas kernels  46.9 us (90%)
  local copies, waits for them, and re-layouts  3.41 us (7%)
  between operations  1.4 us (3%)
    pallas_call x1, Pallas kernels, local(): pl.pallas_call(kernel, name='substep', out_shape=(jax.ShapeDtypeStruct(bl...  46.9 us
    unnamed x7, local copies, waits for them, and re-layouts  3.41 us

profile of v1, /device:TPU:1, one launch (start us, length us, event | category | flops | bytes accessed | tf_op | source)
XLA Modules:
  0.0 51.7 jit_solution(15748932532871738588)
XLA Ops:
  0.6 0.0 copy-start.1
  0.6 0.0 copy-start
  1.4 1.6 %copy.6.op_hbm = f32[512,544]{1,0:T(8,128)S(1)} copy(f32[512,544]{0,1:T(8,128)} %param.5) | data formatting | bytes 2228224 | tf_op args[1]
  3.0 0.0 copy-done.1
  3.0 0.0 copy-done
  3.0 46.9 %substep.1 = (f32[3,16,8,512]{3,2,1,0:T(8,128)S(1)}, f32[3,16,8,512]{3,2,1,0:T(8,128)S(1)}) custom-call(f32[3,16,8,512]{3,2,1,0:T(8,128)S(1)} %copy-done, f32[512,544]{1,0:T(8,128)S(1)} %copy.6.op_hbm, f32[21]{0:T(128)S(1)} %copy-done.1, f32[1]{0:T(128)S(6)} %copy.9.visc), custom_call_target="tpu_custom_call" | custom-call | tf_op jit(solution)/shard_map/substep/pallas_call | solution.py:369
  50.0 0.9 %copy.10 = f32[3,16,8,512]{3,2,1,0:T(8,128)} copy(f32[3,16,8,512]{3,2,1,0:T(8,128)S(1)} %get-tuple-element.4) | data formatting | bytes 1572864
  50.9 0.9 %copy.11 = f32[3,16,8,512]{3,2,1,0:T(8,128)} copy(f32[3,16,8,512]{3,2,1,0:T(8,128)S(1)} %get-tuple-element.5) | data formatting | bytes 1572864
Async XLA Ops:
  0.6 2.4 %copy-start.1 = (f32[21]{0:T(128)S(1)}, f32[21]{0:T(128)}, u32[]{:S(2)}) copy-start(f32[21]{0:T(128)} %sten.1) | copy-start | bytes 256
  0.6 2.4 %copy-start = (f32[3,16,8,512]{3,2,1,0:T(8,128)S(1)}, f32[3,16,8,512]{3,2,1,0:T(8,128)}, u32[]{:S(2)}) copy-start(f32[3,16,8,512]{3,2,1,0:T(8,128)} %v_hbm.1) | copy-start | bytes 2359300

commit v2 on v0

v2 whole, which is shorter than its diff:
```python
import jax
import jax.numpy as jnp
from jax import lax
from jax.experimental import pallas as pl
from jax.experimental.pallas import tpu as pltpu
from jax.sharding import PartitionSpec as P

AXIAL_WEIGHTS = (0.75, -0.15, 1.0 / 60.0)
STEP_WEIGHT = 0.2
MIRROR_SIGNS = (-1.0, -1.0, 1.0)
MESH = pl.DeviceIdType.MESH
F32 = jnp.float32
BF16 = jnp.bfloat16
REACH = 10
PTS = 16
NR = 512
RT = 32
LANES = 128
TILES = NR // LANES
GROUP = 8
SECTORS = 128
BLOCKS = SECTORS // GROUP
PLAIN_DOT = (((1,), (0,)), ((), ()))


def split(x):
    high = x.astype(BF16)
    return high, (x - high.astype(F32)).astype(BF16)


def dot3(x, w_high, w_low):
    high, low = split(x)
    out = lax.dot_general(high, w_low, PLAIN_DOT, preferred_element_type=F32)
    out = out + lax.dot_general(low, w_high, PLAIN_DOT, preferred_element_type=F32)
    return out + lax.dot_general(high, w_high, PLAIN_DOT, preferred_element_type=F32)


def rows_of(shape):
    return lax.broadcasted_iota(jnp.int32, shape, len(shape) - 2)


def lane(shape):
    return lax.broadcasted_iota(jnp.int32, shape, len(shape) - 1)


def doubled(q):
    return q * (2.0 - q)


def pack4(x, sub):
    middle = (sub == 3) | (sub == 4)
    return (
        jnp.where(middle, pltpu.roll(x[3], 3, 0), x[0]),
        jnp.where(sub == 3, pltpu.roll(x[3], 1, 0), jnp.where(sub == 4, pltpu.roll(x[3], 7, 0), x[1])),
        jnp.where(middle, pltpu.roll(x[3], 5, 0), x[2]),
    )


def unpack4(y, sub):
    fourth = jnp.where(
        sub < 2,
        pltpu.roll(y[0], 5, 0),
        jnp.where(
            sub == 2,
            pltpu.roll(y[1], 7, 0),
            jnp.where(sub == 5, pltpu.roll(y[1], 1, 0), pltpu.roll(y[2], 3, 0)),
        ),
    )
    return (y[0], y[1], y[2], fourth)


def axial_parts(x, sub):
    own = far = None
    for m, weight in enumerate(AXIAL_WEIGHTS, 1):
        upper = weight * pltpu.roll(x, 8 - m, 0)
        lower = weight * pltpu.roll(x, m, 0)
        inside = jnp.where(sub < 8 - m, upper, 0.0) - jnp.where(sub >= m, lower, 0.0)
        outside = jnp.where(sub < 8 - m, 0.0, upper) - jnp.where(sub >= m, 0.0, lower)
        own = inside if own is None else own + inside
        far = outside if far is None else far + outside
    return own, far


def kernel(
    v_hbm, op_hbm, sten, visc, new_hbm, non_hbm,
    ext, op_v, wh, wl, esend, erecv, gsend, grecv, msend, mrecv, part, own_ax, far_ax, loc,
    inv_t, pow_t, scale_t, w_t, big_t, inv_n, ssend, srecv, fb, up_in, ret, tot, car,
    in_sem, e_sem, mir_sem, up_sem, down_sem, g_sem, sum_sem, p1_s, p1_r, p2_s, p2_r, p3_s, p3_r, out_sem,
):
    p = lax.axis_index("theta")
    g = lax.axis_index("gz")
    me = p % GROUP
    block = p // GROUP
    backward = me // TILES
    my_tile = me % TILES
    sub = rows_of((8, LANES))

    reads = [
        pltpu.make_async_copy(v_hbm, ext.at[:, pl.ds(REACH, PTS)], in_sem.at[0]),
        pltpu.make_async_copy(op_hbm, op_v, in_sem.at[1]),
    ]
    for r in reads:
        r.start()

    after = (p + 1) % SECTORS
    before = (p + SECTORS - 1) % SECTORS
    across = (p + SECTORS // 2) % SECTORS
    barrier = pltpu.get_barrier_semaphore()
    greeted = [(p, 1 - g), (after, g), (before, g)]
    greeted += [(block * GROUP + (me + k) % GROUP, g) for k in range(1, GROUP)]
    greeted += [(((block + k) % BLOCKS) * GROUP + me, g) for k in range(1, BLOCKS)]
    for who in greeted:
        pl.semaphore_signal(barrier, inc=1, device_id=who, device_id_type=MESH)

    def cols(t):
        return pl.ds(pl.multiple_of(t * LANES, LANES), LANES)

    reads[0].wait()

    def pack_axial(t, carry):
        for i in range(PTS // 4):
            x = [ext[2, REACH + 4 * i + j, :, cols(t)] for j in range(4)]
            for j, y in enumerate(pack4(x, sub)):
                esend[3 * i + j, :, cols(t)] = y
        return carry

    lax.fori_loop(0, TILES, pack_axial, 0)
    quarter = lane((8, LANES)) // RT
    for c in range(3):
        for i in range(PTS // 4):
            line = ext[c, REACH + 4 * i, :, :LANES]
            for j in range(1, 4):
                line = jnp.where(quarter == j, pltpu.roll(ext[c, REACH + 4 * i + j, :, :LANES], RT * j, 1), line)
            msend[c, i] = MIRROR_SIGNS[c] * line

    pl.semaphore_wait(barrier, len(greeted))

    def remote(src, dst, s_sem, r_sem, who):
        return pltpu.make_async_remote_copy(
            src_ref=src, dst_ref=dst, send_sem=s_sem, recv_sem=r_sem, device_id=who, device_id_type=MESH
        )

    def pair(src, dst, sem, who):
        return remote(src, dst, sem.at[0], sem.at[1], who)

    planes_e = pair(esend, erecv, e_sem, (p, 1 - g))
    halo_up = pair(ext.at[:, pl.ds(PTS, REACH)], ext.at[:, pl.ds(0, REACH)], up_sem, (after, g))
    halo_down = pair(ext.at[:, pl.ds(REACH, REACH)], ext.at[:, pl.ds(REACH + PTS, REACH)], down_sem, (before, g))
    mirror = pair(msend, mrecv, mir_sem, (across, g))
    sums = pair(ssend, srecv, sum_sem, (p, 1 - g))
    planes = [
        remote(gsend.at[c], grecv.at[c], g_sem.at[0, c], g_sem.at[1, c], (p, 1 - g)) for c in range(2)
    ]
    planes_e.start()
    halo_up.start()
    halo_down.start()
    mirror.start()

    radius = lane((8, NR)).astype(F32) + 0.5
    inverse_r = 1.0 / radius
    coef = visc[0] * inverse_r * inverse_r
    half = 0.5 / coef
    gap = jnp.sqrt(half * (2.0 + half)) - half
    rho = 1.0 - gap
    scale = 1.0 / jnp.sqrt(1.0 + 4.0 * coef)
    gap16 = doubled(doubled(doubled(doubled(gap))))
    gap128 = doubled(doubled(doubled(gap16)))
    whole = doubled(doubled(doubled(doubled(gap128))))
    for t in range(TILES):
        here = slice(t * LANES, (t + 1) * LANES)
        inv_t[t] = inverse_r[:, here]
        scale_t[t] = scale[:, here]
        w_t[t] = 1.0 - gap16[:, here]
        big_t[t] = 1.0 - gap128[:, here]
        inv_n[t] = 1.0 / whole[:, here]
        power = jnp.ones((8, LANES), F32)
        for j in range(PTS + 1):
            pow_t[t, j] = power
            power = power * rho[:, here]

    def spread(t, carry):
        for c in range(3):
            for i in range(PTS // 4):
                far = []
                for j in range(4):
                    row = 4 * i + j
                    inside, outside = axial_parts(ext[c, REACH + row, :, cols(t)], sub)
                    own_ax[c, row, :, cols(t)] = inside
                    far_ax[c, row, :, cols(t)] = outside
                    far.append(outside)
                if c < 2:
                    for j, y in enumerate(pack4(far, sub)):
                        gsend[c, 3 * i + j, :, cols(t)] = y
        return carry

    lax.fori_loop(0, TILES, spread, 0)

    reads[1].wait()
    op_high, op_low = split(op_v[...])
    wh[...] = op_high
    wl[...] = op_low
    for c in range(3):
        lines = ext[c, pl.ds(REACH, PTS)].reshape(PTS * 8, NR)
        part[c] = dot3(lines, wh[pl.ds(0, NR)], wl[pl.ds(0, NR)]).reshape(PTS, 8, NR)

    planes_e.wait_recv()

    def partner_sums(t, carry):
        rho = pow_t[t, 1]
        e = []
        for i in range(PTS // 4):
            e += unpack4([erecv[3 * i + j, :, cols(t)] for j in range(3)], sub)
        for c in range(3):
            ahead = back = None
            for row in range(PTS):
                x = e[row] * far_ax[c, row, :, cols(t)]
                ahead = x if row == 0 else rho * ahead + x
                back = x if row == 0 else back + pow_t[t, row] * x
            ssend[t, c] = ahead
            ssend[TILES + t, c] = back
        return carry

    lax.fori_loop(0, TILES, partner_sums, 0)
    sums.start()
    for cp in planes:
        cp.start()

    mirror.wait_recv()

    def across_axis(i, carry):
        lines = []
        for c in range(3):
            packed = mrecv[c, i]
            lines += [packed[:, :RT]] + [pltpu.roll(packed, LANES - RT * j, 1)[:, :RT] for j in range(1, 4)]
        more = dot3(jnp.concatenate(lines, axis=0), wh[pl.ds(NR, RT)], wl[pl.ds(NR, RT)]).reshape(3, 4, 8, NR)
        rows = pl.ds(4 * i, 4)
        for c in range(3):
            part[c, rows] = part[c, rows] + more[c]
        return carry

    lax.fori_loop(0, PTS // 4, across_axis, 0)
    halo_up.wait_recv()
    halo_down.wait_recv()

    def azimuth(t, carry):
        inv, rho = inv_t[t], pow_t[t, 1]
        for c in range(3):
            x = [ext[c, k, :, cols(t)] for k in range(PTS + 2 * REACH)]
            ahead = back = None
            for row in range(PTS):
                grad = sten[0] * x[row]
                for m in range(1, 2 * REACH + 1):
                    grad = grad + sten[m] * x[row + m]
                a = ext[0, REACH + row, :, cols(t)]
                b = ext[1, REACH + row, :, cols(t)]
                e = ext[2, REACH + row, :, cols(t)]
                turn = b * inv
                if c == 0:
                    grad = grad - b
                if c == 1:
                    grad = grad + a
                term = a * part[c, row, :, cols(t)] + turn * grad + e * own_ax[c, row, :, cols(t)]
                part[c, row, :, cols(t)] = term
                right = x[REACH + row] - STEP_WEIGHT * term
                ahead = right if row == 0 else rho * ahead + right
                back = right if row == 0 else back + pow_t[t, row] * right
            fb[t, c] = ahead
            fb[TILES + t, c] = back
        return carry

    lax.fori_loop(0, TILES, azimuth, 0)

    sums.wait_recv()
    for k in range(GROUP):
        fb[k] = fb[k] - STEP_WEIGHT * srecv[k]

    one, two, three = [], [], []
    for k in range(1, GROUP):
        other = (me + k) % GROUP
        cp = remote(fb.at[other], up_in.at[me], p1_s.at[k - 1], p1_r.at[k - 1], (block * GROUP + other, g))
        cp.start()
        one.append(cp)
    up_in[me] = fb[me]

    def finish_term(c):
        def body(t, carry):
            rho = pow_t[t, 1]
            right = []
            left = []
            for i in range(PTS // 4):
                if c < 2:
                    far = unpack4([grecv[c, 3 * i + j, :, cols(t)] for j in range(3)], sub)
                else:
                    far = unpack4([erecv[3 * i + j, :, cols(t)] for j in range(3)], sub)
                for j in range(4):
                    row = 4 * i + j
                    grad = far[j]
                    if c == 2:
                        grad = axial_parts(grad, sub)[1]
                    else:
                        grad = jnp.where((sub == 3) | (sub == 4), 0.0, grad)
                    term = part[c, row, :, cols(t)] + ext[2, REACH + row, :, cols(t)] * grad
                    part[c, row, :, cols(t)] = term
                    right.append(ext[c, REACH + row, :, cols(t)] - STEP_WEIGHT * term)
                    left.append(right[row] if row == 0 else right[row] + rho * left[row - 1])
            run = None
            for row in range(PTS - 1, -1, -1):
                if run is None:
                    loc[c, row, :, cols(t)] = left[row]
                    run = right[row]
                else:
                    run = rho * run
                    loc[c, row, :, cols(t)] = left[row] + run
                    run = right[row] + run
            return carry

        lax.fori_loop(0, TILES, body, 0)

    def write(src, dst, k):
        cp = pltpu.make_async_copy(src, dst, out_sem.at[k])
        cp.start()
        return cp

    def entry(k):
        return k + backward * (GROUP - 1 - 2 * k)

    for cp in one:
        cp.wait_recv()
    w = w_t[my_tile]
    run = up_in[entry(0)]
    for k in range(1, GROUP):
        run = up_in[entry(k)] + w * run
    tot[block] = run
    for k in range(1, BLOCKS):
        cp = remote(
            tot.at[block], tot.at[block], p2_s.at[k - 1], p2_r.at[k - 1],
            (((block + k) % BLOCKS) * GROUP + me, g),
        )
        cp.start()
        two.append(cp)

    finish_term(2)
    writes = [write(part.at[2], non_hbm.at[2], 0)]

    for cp in two:
        cp.wait_recv()
    big = big_t[my_tile]
    run = tot[block]
    for m in range(BLOCKS - 1, 0, -1):
        run = tot[(block + (2 * backward - 1) * m + BLOCKS) % BLOCKS] + big * run
    run = run * inv_n[my_tile]
    for k in range(GROUP):
        ret[entry(k)] = run
        run = up_in[entry(k)] + w * run
    for k in range(1, GROUP):
        other = (me + k) % GROUP
        cp = remote(ret.at[other], car.at[me], p3_s.at[k - 1], p3_r.at[k - 1], (block * GROUP + other, g))
        cp.start()
        three.append(cp)
    car[me] = ret[me]

    for c in range(2):
        planes[c].wait_recv()
        finish_term(c)
        writes.append(write(part.at[c], non_hbm.at[c], 1 + c))

    for cp in three:
        cp.wait_recv()

    def last(t, carry):
        scale = scale_t[t]
        for c in range(3):
            from_left = scale * car[t, c]
            from_right = scale * car[TILES + t, c]
            for row in range(PTS):
                loc[c, row, :, cols(t)] = (
                    scale * loc[c, row, :, cols(t)]
                    + pow_t[t, row + 1] * from_left
                    + pow_t[t, PTS - row] * from_right
                )
        return carry

    lax.fori_loop(0, TILES, last, 0)
    writes.append(write(loc, new_hbm, 3))
    for cp in (planes_e, halo_up, halo_down, mirror, sums, *planes, *one, *two, *three):
        cp.wait_send()
    for cp in writes:
        cp.wait()


def local(velocity, radial_op, azimuth_stencil, viscous_factor):
    dma = pltpu.SemaphoreType.DMA
    block = velocity.shape
    any_space = pl.BlockSpec(memory_space=pl.ANY)
    scalars = pl.BlockSpec(memory_space=pltpu.SMEM)
    tile = (8, LANES)
    return pl.pallas_call(
        kernel,
        name="substep",
        out_shape=(jax.ShapeDtypeStruct(block, F32), jax.ShapeDtypeStruct(block, F32)),
        in_specs=[any_space, any_space, scalars, scalars],
        out_specs=(any_space, any_space),
        scratch_shapes=[
            pltpu.VMEM((3, PTS + 2 * REACH, 8, NR), F32),
            pltpu.VMEM((NR + RT, NR), F32),
            pltpu.VMEM((NR + RT, NR), BF16),
            pltpu.VMEM((NR + RT, NR), BF16),
            pltpu.VMEM((12, 8, NR), F32),
            pltpu.VMEM((12, 8, NR), F32),
            pltpu.VMEM((2, 12, 8, NR), F32),
            pltpu.VMEM((2, 12, 8, NR), F32),
            pltpu.VMEM((3, 4, *tile), F32),
            pltpu.VMEM((3, 4, *tile), F32),
            pltpu.VMEM(block, F32),
            pltpu.VMEM(block, F32),
            pltpu.VMEM(block, F32),
            pltpu.VMEM(block, F32),
            pltpu.VMEM((TILES, *tile), F32),
            pltpu.VMEM((TILES, PTS + 1, *tile), F32),
            pltpu.VMEM((TILES, *tile), F32),
            pltpu.VMEM((TILES, *tile), F32),
            pltpu.VMEM((TILES, *tile), F32),
            pltpu.VMEM((TILES, *tile), F32),
            pltpu.VMEM((GROUP, 3, *tile), F32),
            pltpu.VMEM((GROUP, 3, *tile), F32),
            pltpu.VMEM((GROUP, 3, *tile), F32),
            pltpu.VMEM((GROUP, 3, *tile), F32),
            pltpu.VMEM((GROUP, 3, *tile), F32),
            pltpu.VMEM((BLOCKS, 3, *tile), F32),
            pltpu.VMEM((GROUP, 3, *tile), F32),
            dma((2,)),
            dma((2,)), dma((2,)), dma((2,)), dma((2,)),
            dma((2, 2)), dma((2,)),
            dma((GROUP - 1,)), dma((GROUP - 1,)),
            dma((BLOCKS - 1,)), dma((BLOCKS - 1,)),
            dma((GROUP - 1,)), dma((GROUP - 1,)),
            dma((4,)),
        ],
        compiler_params=pltpu.CompilerParams(
            collective_id=0, has_side_effects=True, vmem_limit_bytes=40 << 20
        ),
    )(velocity, radial_op.T, azimuth_stencil, viscous_factor)


def solution(mesh):
    spec = P(None, "theta", "gz", None)
    return jax.shard_map(
        local, mesh=mesh, in_specs=(spec, P(), P(), P()), out_specs=(spec, spec), check_vma=False
    )
```

time: 315 us -> 49.8 us (0.16)
  the two profiles are of different devices: /device:TPU:36 before, /device:TPU:1 now
where the time goes in v2:
time: 49.8 us; the launch traced here: 49.6 us
  Pallas kernels  43.6 us (88%)
  local copies, waits for them, and re-layouts  4.79 us (10%)
  between operations  1.3 us (3%)
    pallas_call x1, Pallas kernels, local(): pl.pallas_call(kernel, name='substep', out_shape=(jax.ShapeDtypeStruct(bl...  43.6 us
    unnamed x8, local copies, waits for them, and re-layouts  4.79 us

profile of v2, /device:TPU:1, one launch (start us, length us, event | category | flops | bytes accessed | tf_op | source)
XLA Modules:
  0.0 49.6 jit_solution(9615513956397161333)
XLA Ops:
  1.3 0.0 copy-start
  1.3 1.2 %copy-done = f32[512,544]{0,1:T(8,128)S(1)} copy-done((f32[512,544]{0,1:T(8,128)S(1)}, f32[512,544]{0,1:T(8,128)}, u32[]{:S(2)}) %copy-start) | copy-done | bytes 1114136
  2.5 0.0 copy-start.1
  2.5 1.1 %copy-done.1 = f32[3,16,8,512]{3,2,1,0:T(8,128)S(1)} copy-done((f32[3,16,8,512]{3,2,1,0:T(8,128)S(1)}, f32[3,16,8,512]{3,2,1,0:T(8,128)}, u32[]{:S(2)}) %copy-start.1) | copy-done | bytes 786456
  3.7 0.0 copy-start.2
  3.7 0.7 %copy-done.2 = f32[21]{0:T(128)S(1)} copy-done((f32[21]{0:T(128)S(1)}, f32[21]{0:T(128)}, u32[]{:S(2)}) %copy-start.2) | copy-done | bytes 108
  4.3 43.6 %substep.1 = (f32[3,16,8,512]{3,2,1,0:T(8,128)S(1)}, f32[3,16,8,512]{3,2,1,0:T(8,128)S(1)}) custom-call(f32[3,16,8,512]{3,2,1,0:T(8,128)S(1)} %copy-done.1, f32[544,512]{1,0:T(8,128)S(1)} %bitcast.1, f32[21]{0:T(128)S(1)} %copy-done.2, f32[1]{0:T(128)S(6)} %copy.8.visc), custom_call_target="tpu_custom_call" | custom-call | tf_op jit(solution)/shard_map/substep/pallas_call | solution.py:397
  47.9 0.9 %copy.9 = f32[3,16,8,512]{3,2,1,0:T(8,128)} copy(f32[3,16,8,512]{3,2,1,0:T(8,128)S(1)} %get-tuple-element.4) | data formatting | bytes 1572864
  48.8 0.9 %copy.10 = f32[3,16,8,512]{3,2,1,0:T(8,128)} copy(f32[3,16,8,512]{3,2,1,0:T(8,128)S(1)} %get-tuple-element.5) | data formatting | bytes 1572864
Async XLA Ops:
  1.3 1.2 %copy-start = (f32[512,544]{0,1:T(8,128)S(1)}, f32[512,544]{0,1:T(8,128)}, u32[]{:S(2)}) copy-start(f32[512,544]{0,1:T(8,128)} %param.5) | copy-start | bytes 3342340
  2.5 1.1 %copy-start.1 = (f32[3,16,8,512]{3,2,1,0:T(8,128)S(1)}, f32[3,16,8,512]{3,2,1,0:T(8,128)}, u32[]{:S(2)}) copy-start(f32[3,16,8,512]{3,2,1,0:T(8,128)} %v_hbm.1) | copy-start | bytes 2359300
  3.7 0.7 %copy-start.2 = (f32[21]{0:T(128)S(1)}, f32[21]{0:T(128)}, u32[]{:S(2)}) copy-start(f32[21]{0:T(128)} %sten.1) | copy-start | bytes 256

commit v3 on v2

--- a/solution.py
+++ b/solution.py
@@ -20,6 +20,7 @@
 GROUP = 8
 SECTORS = 128
 BLOCKS = SECTORS // GROUP
+ROWS = (range(0, REACH), range(PTS - REACH, PTS))
 PLAIN_DOT = (((1,), (0,)), ((), ()))
 
 
@@ -84,8 +85,9 @@
 def kernel(
     v_hbm, op_hbm, sten, visc, new_hbm, non_hbm,
     ext, op_v, wh, wl, esend, erecv, gsend, grecv, msend, mrecv, part, own_ax, far_ax, loc,
-    inv_t, pow_t, scale_t, w_t, big_t, inv_n, ssend, srecv, fb, up_in, ret, tot, car,
-    in_sem, e_sem, mir_sem, up_sem, down_sem, g_sem, sum_sem, p1_s, p1_r, p2_s, p2_r, p3_s, p3_r, out_sem,
+    inv_t, pow_t, scale_t, w_t, big_t, inv_n, ssend, sum_in, hsend, halo_in, fb, up_in, ret, tot, car,
+    in_sem, e_sem, mir_sem, up_sem, down_sem, g_sem, v_s, v_r, h_s, h_r,
+    p1_s, p1_r, p2_s, p2_r, p3_s, p3_r, out_sem,
 ):
     p = lax.axis_index("theta")
     g = lax.axis_index("gz")
@@ -106,9 +108,12 @@
     before = (p + SECTORS - 1) % SECTORS
     across = (p + SECTORS // 2) % SECTORS
     barrier = pltpu.get_barrier_semaphore()
-    greeted = [(p, 1 - g), (after, g), (before, g)]
+    greeted = [(after, g), (before, g)]
     greeted += [(block * GROUP + (me + k) % GROUP, g) for k in range(1, GROUP)]
+    greeted += [(block * GROUP + (me + k) % GROUP, 1 - g) for k in range(GROUP)]
     greeted += [(((block + k) % BLOCKS) * GROUP + me, g) for k in range(1, BLOCKS)]
+    greeted += [(((block + BLOCKS - 1) % BLOCKS) * GROUP + GROUP - 1, g), (((block + 1) % BLOCKS) * GROUP, g)]
+    at_edge = me // (GROUP - 1) + (GROUP - 1 - me) // (GROUP - 1)
     for who in greeted:
         pl.semaphore_signal(barrier, inc=1, device_id=who, device_id_type=MESH)
 
@@ -133,7 +138,7 @@
                 line = jnp.where(quarter == j, pltpu.roll(ext[c, REACH + 4 * i + j, :, :LANES], RT * j, 1), line)
             msend[c, i] = MIRROR_SIGNS[c] * line
 
-    pl.semaphore_wait(barrier, len(greeted))
+    pl.semaphore_wait(barrier, len(greeted) - 2 + GROUP * at_edge)
 
     def remote(src, dst, s_sem, r_sem, who):
         return pltpu.make_async_remote_copy(
@@ -144,17 +149,42 @@
         return remote(src, dst, sem.at[0], sem.at[1], who)
 
     planes_e = pair(esend, erecv, e_sem, (p, 1 - g))
-    halo_up = pair(ext.at[:, pl.ds(PTS, REACH)], ext.at[:, pl.ds(0, REACH)], up_sem, (after, g))
-    halo_down = pair(ext.at[:, pl.ds(REACH, REACH)], ext.at[:, pl.ds(REACH + PTS, REACH)], down_sem, (before, g))
+    halo_up, halo_down = [], []
+    for c in range(3):
+        halo_up.append(
+            remote(ext.at[c, pl.ds(PTS, REACH)], ext.at[c, pl.ds(0, REACH)], up_sem.at[0, c], up_sem.at[1, c], (after, g))
+        )
+        halo_down.append(
+            remote(
+                ext.at[c, pl.ds(REACH, REACH)], ext.at[c, pl.ds(REACH + PTS, REACH)],
+                down_sem.at[0, c], down_sem.at[1, c], (before, g),
+            )
+        )
     mirror = pair(msend, mrecv, mir_sem, (across, g))
-    sums = pair(ssend, srecv, sum_sem, (p, 1 - g))
+    sums = []
+    for k in range(GROUP):
+        other = (me + k) % GROUP
+        sums.append(
+            remote(ssend.at[other], sum_in.at[me], v_s.at[k], v_r.at[k], (block * GROUP + other, 1 - g))
+        )
     planes = [
         remote(gsend.at[c], grecv.at[c], g_sem.at[0, c], g_sem.at[1, c], (p, 1 - g)) for c in range(2)
     ]
+    first, final = me == 0, me == GROUP - 1
     planes_e.start()
-    halo_up.start()
-    halo_down.start()
+    halo_up[1].start()
+    halo_down[1].start()
     mirror.start()
+
+    @pl.when(me != GROUP - 1)
+    def _():
+        halo_up[0].start()
+        halo_up[2].start()
+
+    @pl.when(me != 0)
+    def _():
+        halo_down[0].start()
+        halo_down[2].start()
 
     radius = lane((8, NR)).astype(F32) + 0.5
     inverse_r = 1.0 / radius
@@ -203,6 +233,29 @@
         lines = ext[c, pl.ds(REACH, PTS)].reshape(PTS * 8, NR)
         part[c] = dot3(lines, wh[pl.ds(0, NR)], wl[pl.ds(0, NR)]).reshape(PTS, 8, NR)
 
+    def azimuth(t, carry):
+        inv = inv_t[t]
+        for c in range(3):
+            x = [ext[c, REACH + k, :, cols(t)] for k in range(PTS)]
+            for row in range(PTS):
+                grad = None
+                for k in range(max(0, row - REACH), min(PTS, row + REACH + 1)):
+                    tap = sten[k - row + REACH] * x[k]
+                    grad = tap if grad is None else grad + tap
+                a = ext[0, REACH + row, :, cols(t)]
+                b = ext[1, REACH + row, :, cols(t)]
+                e = ext[2, REACH + row, :, cols(t)]
+                if c == 0:
+                    grad = grad - b
+                if c == 1:
+                    grad = grad + a
+                part[c, row, :, cols(t)] = (
+                    a * part[c, row, :, cols(t)] + (b * inv) * grad + e * own_ax[c, row, :, cols(t)]
+                )
+        return carry
+
+    lax.fori_loop(0, TILES, azimuth, 0)
+
     planes_e.wait_recv()
 
     def partner_sums(t, carry):
@@ -216,14 +269,77 @@
                 x = e[row] * far_ax[c, row, :, cols(t)]
                 ahead = x if row == 0 else rho * ahead + x
                 back = x if row == 0 else back + pow_t[t, row] * x
-            ssend[t, c] = ahead
-            ssend[TILES + t, c] = back
+            ssend[t, c] = -STEP_WEIGHT * ahead
+            ssend[TILES + t, c] = -STEP_WEIGHT * back
         return carry
 
     lax.fori_loop(0, TILES, partner_sums, 0)
-    sums.start()
+    for cp in sums:
+        cp.start()
+
+    def halo_taps(t, c, row, shift):
+        span = range(row, REACH) if shift[0] == 0 else range(REACH + PTS, row + 2 * REACH + 1)
+        grad = None
+        for k in span:
+            tap = sten[k - row] * ext[c, k + shift[1], :, cols(t)]
+            grad = tap if grad is None else grad + tap
+        return grad
+
+    def edge_sums(side):
+        shift = (side, PTS if side == 0 else -PTS)
+        theirs = REACH + PTS if side == 0 else REACH - PTS
+
+        def body(t, carry):
+            inv, rho = inv_t[t], pow_t[t, 1]
+            for c in range(3):
+                ahead = back = None
+                for row in ROWS[side]:
+                    x = (ext[1, row + theirs, :, cols(t)] * inv) * halo_taps(t, c, row, shift)
+                    ahead = x if ahead is None else rho * ahead + x
+                    x = pow_t[t, row] * x
+                    back = x if back is None else back + x
+                if side == 0:
+                    ahead = ahead * pow_t[t, PTS - REACH]
+                hsend[t, c] = -STEP_WEIGHT * ahead
+                hsend[TILES + t, c] = -STEP_WEIGHT * back
+            return carry
+
+        lax.fori_loop(0, TILES, body, 0)
+
+    def edge_copies(side):
+        to = (block + 1) % BLOCKS if side == 0 else (block + BLOCKS - 1) % BLOCKS
+        return [
+            remote(hsend.at[k], halo_in.at[side], h_s.at[k], h_r.at[side], (to * GROUP + k, g)) for k in range(GROUP)
+        ]
+
+    edge = [edge_copies(0), edge_copies(1)]
+
+    @pl.when(final)
+    def _():
+        halo_down[1].wait_recv()
+        edge_sums(0)
+        for cp in edge[0]:
+            cp.start()
+
+    @pl.when(first)
+    def _():
+        halo_up[1].wait_recv()
+        edge_sums(1)
+        for cp in edge[1]:
+            cp.start()
+
     for cp in planes:
         cp.start()
+
+    @pl.when(final)
+    def _():
+        halo_up[0].start()
+        halo_up[2].start()
+
+    @pl.when(first)
+    def _():
+        halo_down[0].start()
+        halo_down[2].start()
 
     mirror.wait_recv()
 
@@ -235,44 +351,57 @@
         more = dot3(jnp.concatenate(lines, axis=0), wh[pl.ds(NR, RT)], wl[pl.ds(NR, RT)]).reshape(3, 4, 8, NR)
         rows = pl.ds(4 * i, 4)
         for c in range(3):
-            part[c, rows] = part[c, rows] + more[c]
+            part[c, rows] = part[c, rows] + ext[0, pl.ds(REACH + 4 * i, 4)] * more[c]
         return carry
 
     lax.fori_loop(0, PTS // 4, across_axis, 0)
-    halo_up.wait_recv()
-    halo_down.wait_recv()
-
-    def azimuth(t, carry):
-        inv, rho = inv_t[t], pow_t[t, 1]
+
+    def local_sums(t, carry):
+        rho = pow_t[t, 1]
         for c in range(3):
-            x = [ext[c, k, :, cols(t)] for k in range(PTS + 2 * REACH)]
             ahead = back = None
             for row in range(PTS):
-                grad = sten[0] * x[row]
-                for m in range(1, 2 * REACH + 1):
-                    grad = grad + sten[m] * x[row + m]
-                a = ext[0, REACH + row, :, cols(t)]
-                b = ext[1, REACH + row, :, cols(t)]
-                e = ext[2, REACH + row, :, cols(t)]
-                turn = b * inv
-                if c == 0:
-                    grad = grad - b
-                if c == 1:
-                    grad = grad + a
-                term = a * part[c, row, :, cols(t)] + turn * grad + e * own_ax[c, row, :, cols(t)]
-                part[c, row, :, cols(t)] = term
-                right = x[REACH + row] - STEP_WEIGHT * term
+                right = ext[c, REACH + row, :, cols(t)] - STEP_WEIGHT * part[c, row, :, cols(t)]
                 ahead = right if row == 0 else rho * ahead + right
                 back = right if row == 0 else back + pow_t[t, row] * right
             fb[t, c] = ahead
             fb[TILES + t, c] = back
         return carry
 
-    lax.fori_loop(0, TILES, azimuth, 0)
-
-    sums.wait_recv()
-    for k in range(GROUP):
-        fb[k] = fb[k] - STEP_WEIGHT * srecv[k]
+    lax.fori_loop(0, TILES, local_sums, 0)
+
+    def add_halo(side, summed):
+        def body(t, carry):
+            inv, rho = inv_t[t], pow_t[t, 1]
+            for c in range(3):
+                ahead = back = None
+                for row in ROWS[side]:
+                    x = (ext[1, REACH + row, :, cols(t)] * inv) * halo_taps(t, c, row, (side, 0))
+                    part[c, row, :, cols(t)] = part[c, row, :, cols(t)] + x
+                    if summed:
+                        ahead = x if ahead is None else rho * ahead + x
+                        x = pow_t[t, row] * x
+                        back = x if back is None else back + x
+                if summed:
+                    if side == 0:
+                        ahead = ahead * pow_t[t, PTS - REACH]
+                    fb[t, c] = fb[t, c] - STEP_WEIGHT * ahead
+                    fb[TILES + t, c] = fb[TILES + t, c] - STEP_WEIGHT * back
+            return carry
+
+        lax.fori_loop(0, TILES, body, 0)
+
+    @pl.when(me != 0)
+    def _():
+        for cp in (halo_up[1], halo_up[0], halo_up[2]):
+            cp.wait_recv()
+        add_halo(0, True)
+
+    @pl.when(me != GROUP - 1)
+    def _():
+        for cp in (halo_down[1], halo_down[0], halo_down[2]):
+            cp.wait_recv()
+        add_halo(1, True)
 
     one, two, three = [], [], []
     for k in range(1, GROUP):
@@ -324,8 +453,15 @@
     def entry(k):
         return k + backward * (GROUP - 1 - 2 * k)
 
-    for cp in one:
+    for cp in (*one, *sums, edge[0][0], edge[1][0]):
         cp.wait_recv()
+    for k in range(GROUP):
+        total = up_in[k] + sum_in[k]
+        if k == 0:
+            total = total + halo_in[0]
+        if k == GROUP - 1:
+            total = total + halo_in[1]
+        up_in[k] = total
     w = w_t[my_tile]
     run = up_in[entry(0)]
     for k in range(1, GROUP):
@@ -338,6 +474,18 @@
         )
         cp.start()
         two.append(cp)
+
+    @pl.when(first)
+    def _():
+        halo_up[0].wait_recv()
+        halo_up[2].wait_recv()
+        add_halo(0, False)
+
+    @pl.when(final)
+    def _():
+        halo_down[0].wait_recv()
+        halo_down[2].wait_recv()
+        add_halo(1, False)
 
     finish_term(2)
     writes = [write(part.at[2], non_hbm.at[2], 0)]
@@ -382,8 +530,16 @@
 
     lax.fori_loop(0, TILES, last, 0)
     writes.append(write(loc, new_hbm, 3))
-    for cp in (planes_e, halo_up, halo_down, mirror, sums, *planes, *one, *two, *three):
+    for cp in (planes_e, *halo_up, *halo_down, mirror, *sums, *planes, *one, *two, *three):
         cp.wait_send()
+
+    for side, here in ((0, final), (1, first)):
+
+        @pl.when(here)
+        def _(side=side):
+            for cp in edge[side]:
+                cp.wait_send()
+
     for cp in writes:
         cp.wait()
 
@@ -424,20 +580,22 @@
             pltpu.VMEM((GROUP, 3, *tile), F32),
             pltpu.VMEM((GROUP, 3, *tile), F32),
             pltpu.VMEM((GROUP, 3, *tile), F32),
+            pltpu.VMEM((2, 3, *tile), F32),
+            pltpu.VMEM((GROUP, 3, *tile), F32),
             pltpu.VMEM((GROUP, 3, *tile), F32),
             pltpu.VMEM((GROUP, 3, *tile), F32),
             pltpu.VMEM((BLOCKS, 3, *tile), F32),
             pltpu.VMEM((GROUP, 3, *tile), F32),
             dma((2,)),
-            dma((2,)), dma((2,)), dma((2,)), dma((2,)),
-            dma((2, 2)), dma((2,)),
+            dma((2,)), dma((2,)), dma((2, 3)), dma((2, 3)),
+            dma((2, 2)), dma((GROUP,)), dma((GROUP,)), dma((GROUP,)), dma((2,)),
             dma((GROUP - 1,)), dma((GROUP - 1,)),
             dma((BLOCKS - 1,)), dma((BLOCKS - 1,)),
             dma((GROUP - 1,)), dma((GROUP - 1,)),
             dma((4,)),
         ],
         compiler_params=pltpu.CompilerParams(
-            collective_id=0, has_side_effects=True, vmem_limit_bytes=40 << 20
+            collective_id=0, has_side_effects=True, vmem_limit_bytes=52 << 20
         ),
     )(velocity, radial_op.T, azimuth_stencil, viscous_factor)
 

time: 49.8 us -> 45.1 us (0.906)
  local copies, waits for them, and re-layouts: 4.79 us -> 2.41 us
  Pallas kernels: 43.6 us -> 41.3 us
    unnamed x8 -> x4, local copies, waits for them, and re-layouts: 4.79 us -> 2.41 us
    pallas_call x1, Pallas kernels: 43.6 us -> 41.3 us  [local(): pl.pallas_call(kernel, name='substep', out_shape=(jax.ShapeDtypeStruct(bl...]
where the time goes in v3:
time: 45.1 us; the launch traced here: 45 us
  Pallas kernels  41.3 us (92%)
  local copies, waits for them, and re-layouts  2.41 us (5%)
  between operations  1.29 us (3%)
    pallas_call x1, Pallas kernels, local(): pl.pallas_call(kernel, name='substep', out_shape=(jax.ShapeDtypeStruct(bl...  41.3 us
    unnamed x4, local copies, waits for them, and re-layouts  2.41 us

profile of v3, /device:TPU:1, one launch (start us, length us, event | category | flops | bytes accessed | tf_op | source)
XLA Modules:
  0.0 45.0 jit_solution(15034590037521415645)
XLA Ops:
  1.3 0.0 copy-start
  1.3 0.6 %copy-done = f32[21]{0:T(128)S(1)} copy-done((f32[21]{0:T(128)S(1)}, f32[21]{0:T(128)}, u32[]{:S(2)}) %copy-start) | copy-done | bytes 108
  1.9 41.3 %substep.1 = (f32[3,16,8,512]{3,2,1,0:T(8,128)S(1)}, f32[3,16,8,512]{3,2,1,0:T(8,128)S(1)}) custom-call(f32[3,16,8,512]{3,2,1,0:T(8,128)} %v_hbm.1, f32[544,512]{1,0:T(8,128)} %bitcast.1, f32[21]{0:T(128)S(1)} %copy-done, f32[1]{0:T(128)S(6)} %copy.8.visc), custom_call_target="tpu_custom_call" | custom-call | tf_op jit(solution)/shard_map/substep/pallas_call | solution.py:553
  43.3 0.9 %copy.9 = f32[3,16,8,512]{3,2,1,0:T(8,128)} copy(f32[3,16,8,512]{3,2,1,0:T(8,128)S(1)} %get-tuple-element.4) | data formatting | bytes 1572864
  44.1 0.9 %copy.10 = f32[3,16,8,512]{3,2,1,0:T(8,128)} copy(f32[3,16,8,512]{3,2,1,0:T(8,128)S(1)} %get-tuple-element.5) | data formatting | bytes 1572864
Async XLA Ops:
  1.3 0.7 %copy-start = (f32[21]{0:T(128)S(1)}, f32[21]{0:T(128)}, u32[]{:S(2)}) copy-start(f32[21]{0:T(128)} %sten.1) | copy-start | bytes 256

commit v4 on v3

--- a/solution.py
+++ b/solution.py
@@ -83,11 +83,12 @@
 
 
 def kernel(
-    v_hbm, op_hbm, sten, visc, new_hbm, non_hbm,
+    v_hbm, op_hbm, sten_hbm, visc, new_hbm, non_hbm,
+    sten,
     ext, op_v, wh, wl, esend, erecv, gsend, grecv, msend, mrecv, part, own_ax, far_ax, loc,
     inv_t, pow_t, scale_t, w_t, big_t, inv_n, ssend, sum_in, hsend, halo_in, fb, up_in, ret, tot, car,
     in_sem, e_sem, mir_sem, up_sem, down_sem, g_sem, v_s, v_r, h_s, h_r,
-    p1_s, p1_r, p2_s, p2_r, p3_s, p3_r, out_sem,
+    p1_s, p1_r, p2_s, p2_r, p3_s, p3_r, out_sem, chain,
 ):
     p = lax.axis_index("theta")
     g = lax.axis_index("gz")
@@ -100,6 +101,7 @@
     reads = [
         pltpu.make_async_copy(v_hbm, ext.at[:, pl.ds(REACH, PTS)], in_sem.at[0]),
         pltpu.make_async_copy(op_hbm, op_v, in_sem.at[1]),
+        pltpu.make_async_copy(sten_hbm, sten, in_sem.at[2]),
     ]
     for r in reads:
         r.start()
@@ -110,10 +112,10 @@
     barrier = pltpu.get_barrier_semaphore()
     greeted = [(after, g), (before, g)]
     greeted += [(block * GROUP + (me + k) % GROUP, g) for k in range(1, GROUP)]
-    greeted += [(block * GROUP + (me + k) % GROUP, 1 - g) for k in range(GROUP)]
-    greeted += [(((block + k) % BLOCKS) * GROUP + me, g) for k in range(1, BLOCKS)]
-    greeted += [(((block + BLOCKS - 1) % BLOCKS) * GROUP + GROUP - 1, g), (((block + 1) % BLOCKS) * GROUP, g)]
-    at_edge = me // (GROUP - 1) + (GROUP - 1 - me) // (GROUP - 1)
+    greeted += [(p, 1 - g)]
+    hop = [((p + d) % SECTORS, g) for d in (2 * GROUP, SECTORS - 2 * GROUP, 4 * GROUP, SECTORS - 4 * GROUP)]
+    side_block = (block + 1 - 2 * (block % 2)) * GROUP + me
+    greeted += [*hop[:2], (side_block, g)]
     for who in greeted:
         pl.semaphore_signal(barrier, inc=1, device_id=who, device_id_type=MESH)
 
@@ -138,7 +140,13 @@
                 line = jnp.where(quarter == j, pltpu.roll(ext[c, REACH + 4 * i + j, :, :LANES], RT * j, 1), line)
             msend[c, i] = MIRROR_SIGNS[c] * line
 
-    pl.semaphore_wait(barrier, len(greeted) - 2 + GROUP * at_edge)
+    pl.semaphore_wait(barrier, len(greeted))
+
+    def tell(stage, whom):
+        for who in whom:
+            pl.semaphore_signal(chain.at[stage], inc=1, device_id=who, device_id_type=MESH)
+
+    tell(0, hop[:2])
 
     def remote(src, dst, s_sem, r_sem, who):
         return pltpu.make_async_remote_copy(
@@ -174,7 +182,6 @@
     planes_e.start()
     halo_up[1].start()
     halo_down[1].start()
-    mirror.start()
 
     @pl.when(me != GROUP - 1)
     def _():
@@ -186,6 +193,7 @@
         halo_down[0].start()
         halo_down[2].start()
 
+    reads[2].wait()
     radius = lane((8, NR)).astype(F32) + 0.5
     inverse_r = 1.0 / radius
     coef = visc[0] * inverse_r * inverse_r
@@ -225,6 +233,9 @@
 
     lax.fori_loop(0, TILES, spread, 0)
 
+    pl.semaphore_wait(chain.at[0], 2)
+    tell(1, hop[2:])
+
     reads[1].wait()
     op_high, op_low = split(op_v[...])
     wh[...] = op_high
@@ -232,6 +243,10 @@
     for c in range(3):
         lines = ext[c, pl.ds(REACH, PTS)].reshape(PTS * 8, NR)
         part[c] = dot3(lines, wh[pl.ds(0, NR)], wl[pl.ds(0, NR)]).reshape(PTS, 8, NR)
+
+    pl.semaphore_wait(chain.at[1], 2)
+    mirror.start()
+    tell(2, [(side_block, g)])
 
     def azimuth(t, carry):
         inv = inv_t[t]
@@ -404,7 +419,7 @@
         add_halo(1, True)
 
     one, two, three = [], [], []
-    for k in range(1, GROUP):
+    for k in sorted(range(1, GROUP), key=lambda k: abs(k - GROUP // 2)):
         other = (me + k) % GROUP
         cp = remote(fb.at[other], up_in.at[me], p1_s.at[k - 1], p1_r.at[k - 1], (block * GROUP + other, g))
         cp.start()
@@ -453,6 +468,7 @@
     def entry(k):
         return k + backward * (GROUP - 1 - 2 * k)
 
+    pl.semaphore_wait(chain.at[2], 1)
     for cp in (*one, *sums, edge[0][0], edge[1][0]):
         cp.wait_recv()
     for k in range(GROUP):
@@ -467,7 +483,7 @@
     for k in range(1, GROUP):
         run = up_in[entry(k)] + w * run
     tot[block] = run
-    for k in range(1, BLOCKS):
+    for k in sorted(range(1, BLOCKS), key=lambda k: abs(k - BLOCKS // 2)):
         cp = remote(
             tot.at[block], tot.at[block], p2_s.at[k - 1], p2_r.at[k - 1],
             (((block + k) % BLOCKS) * GROUP + me, g),
@@ -500,7 +516,7 @@
     for k in range(GROUP):
         ret[entry(k)] = run
         run = up_in[entry(k)] + w * run
-    for k in range(1, GROUP):
+    for k in sorted(range(1, GROUP), key=lambda k: abs(k - GROUP // 2)):
         other = (me + k) % GROUP
         cp = remote(ret.at[other], car.at[me], p3_s.at[k - 1], p3_r.at[k - 1], (block * GROUP + other, g))
         cp.start()
@@ -544,19 +560,34 @@
         cp.wait()
 
 
+def write_out(new_in, non_in, new_out, non_out, sem):
+    copies = []
+    for k, (src, dst) in enumerate(((new_in, new_out), (non_in, non_out))):
+        for c in range(3):
+            copies.append(pltpu.make_async_copy(src.at[c], dst.at[c], sem.at[k, c]))
+    for cp in copies:
+        cp.start()
+    for cp in copies:
+        cp.wait()
+
+
 def local(velocity, radial_op, azimuth_stencil, viscous_factor):
     dma = pltpu.SemaphoreType.DMA
     block = velocity.shape
     any_space = pl.BlockSpec(memory_space=pl.ANY)
-    scalars = pl.BlockSpec(memory_space=pltpu.SMEM)
+    in_place = [
+        pltpu.with_memory_space_constraint(x, pltpu.HBM) for x in (velocity, radial_op.T, azimuth_stencil)
+    ]
     tile = (8, LANES)
-    return pl.pallas_call(
+    shapes = (jax.ShapeDtypeStruct(block, F32), jax.ShapeDtypeStruct(block, F32))
+    outs = pl.pallas_call(
         kernel,
         name="substep",
-        out_shape=(jax.ShapeDtypeStruct(block, F32), jax.ShapeDtypeStruct(block, F32)),
-        in_specs=[any_space, any_space, scalars, scalars],
+        out_shape=shapes,
+        in_specs=[any_space] * 3 + [pl.BlockSpec(memory_space=pltpu.SMEM)],
         out_specs=(any_space, any_space),
         scratch_shapes=[
+            pltpu.SMEM((2 * REACH + 1,), F32),
             pltpu.VMEM((3, PTS + 2 * REACH, 8, NR), F32),
             pltpu.VMEM((NR + RT, NR), F32),
             pltpu.VMEM((NR + RT, NR), BF16),
@@ -586,18 +617,27 @@
             pltpu.VMEM((GROUP, 3, *tile), F32),
             pltpu.VMEM((BLOCKS, 3, *tile), F32),
             pltpu.VMEM((GROUP, 3, *tile), F32),
-            dma((2,)),
+            dma((4,)),
             dma((2,)), dma((2,)), dma((2, 3)), dma((2, 3)),
             dma((2, 2)), dma((GROUP,)), dma((GROUP,)), dma((GROUP,)), dma((2,)),
             dma((GROUP - 1,)), dma((GROUP - 1,)),
             dma((BLOCKS - 1,)), dma((BLOCKS - 1,)),
             dma((GROUP - 1,)), dma((GROUP - 1,)),
             dma((4,)),
+            pltpu.SemaphoreType.REGULAR((3,)),
         ],
         compiler_params=pltpu.CompilerParams(
-            collective_id=0, has_side_effects=True, vmem_limit_bytes=52 << 20
+            collective_id=0, has_side_effects=True, vmem_limit_bytes=40 << 20
         ),
-    )(velocity, radial_op.T, azimuth_stencil, viscous_factor)
+    )(*in_place, viscous_factor)
+    return pl.pallas_call(
+        write_out,
+        name="write_out",
+        out_shape=(pltpu.HBM(block, F32), pltpu.HBM(block, F32)),
+        in_specs=[pl.BlockSpec(memory_space=pltpu.VMEM)] * 2,
+        out_specs=(any_space, any_space),
+        scratch_shapes=[dma((2, 3))],
+    )(*[pltpu.with_memory_space_constraint(x, pltpu.VMEM) for x in outs])
 
 
 def solution(mesh):

time: 45.1 us -> 42 us (0.931)
  local copies, waits for them, and re-layouts: 2.41 us -> 0 us
  Pallas kernels: 41.3 us -> 40.6 us
    unnamed x4 -> x0, local copies, waits for them, and re-layouts: 2.41 us -> none
    pallas_call x1 -> x2, Pallas kernels: 41.3 us -> 40.6 us  [the longest x1 39.4 us: local(): pl.pallas_call(kernel, name='substep', out_shape=shapes, in_specs=[any_sp...]
where the time goes in v4:
time: 42 us; the launch traced here: 41.9 us
  Pallas kernels  40.6 us (97%)
  between operations  1.28 us (3%)
    pallas_call x1, Pallas kernels, local(): pl.pallas_call(kernel, name='substep', out_shape=shapes, in_specs=[any_sp...  39.4 us
    pallas_call x1, Pallas kernels, local(): pl.pallas_call(write_out, name='write_out', out_shape=(pltpu.HBM(block, F...  1.19 us

profile of v4, /device:TPU:1, one launch (start us, length us, event | category | flops | bytes accessed | tf_op | source)
XLA Modules:
  0.0 41.9 jit_solution(13522136930777617787)
XLA Ops:
  1.3 39.4 %substep.1 = (f32[3,16,8,512]{3,2,1,0:T(8,128)S(1)}, f32[3,16,8,512]{3,2,1,0:T(8,128)S(1)}) custom-call(f32[3,16,8,512]{3,2,1,0:T(8,128)} %v_hbm.1, f32[544,512]{1,0:T(8,128)} %bitcast.1, f32[21]{0:T(128)} %sten_hbm.1, f32[1]{0:T(128)S(6)} %copy.6.visc), custom_call_target="tpu_custom_call" | custom-call | tf_op jit(solution)/shard_map/substep/pallas_call | solution.py:583
  40.7 1.2 %write_out.1 = (f32[3,16,8,512]{3,2,1,0:T(8,128)}, f32[3,16,8,512]{3,2,1,0:T(8,128)}) custom-call(f32[3,16,8,512]{3,2,1,0:T(8,128)S(1)} %get-tuple-element.4.new_in, f32[3,16,8,512]{3,2,1,0:T(8,128)S(1)} %get-tuple-element.5.non_in), custom_call_target="tpu_custom_call" | custom-call | tf_op jit(solution)/shard_map/write_out/pallas_call | solution.py:633

commit v5 on v4

--- a/solution.py
+++ b/solution.py
@@ -21,6 +21,7 @@
 SECTORS = 128
 BLOCKS = SECTORS // GROUP
 ROWS = (range(0, REACH), range(PTS - REACH, PTS))
+RELAY = (5, 2)
 PLAIN_DOT = (((1,), (0,)), ((), ()))
 
 
@@ -83,12 +84,12 @@
 
 
 def kernel(
-    v_hbm, op_hbm, sten_hbm, visc, new_hbm, non_hbm,
+    v_hbm, op_hbm, sten_hbm, visc, loc, part, ends, pow_t, scale_t,
     sten,
-    ext, op_v, wh, wl, esend, erecv, gsend, grecv, msend, mrecv, part, own_ax, far_ax, loc,
-    inv_t, pow_t, scale_t, w_t, big_t, inv_n, ssend, sum_in, hsend, halo_in, fb, up_in, ret, tot, car,
+    ext, op_v, wh, wl, esend, erecv, gsend, grecv, msend, mrecv, own_ax, far_ax,
+    inv_t, w_t, big_t, inv_n, ssend, sum_in, hsend, halo_in, fb, up_in, ret, tot, car,
     in_sem, e_sem, mir_sem, up_sem, down_sem, g_sem, v_s, v_r, h_s, h_r,
-    p1_s, p1_r, p2_s, p2_r, p3_s, p3_r, out_sem, chain,
+    p1_s, p1_r, p2_s, p2_r, p3_s, p3_r, relay_in, relay_out, passing, chain,
 ):
     p = lax.axis_index("theta")
     g = lax.axis_index("gz")
@@ -168,6 +169,16 @@
                 down_sem.at[0, c], down_sem.at[1, c], (before, g),
             )
         )
+    next_block, last_block = (block + 1) % BLOCKS, (block + BLOCKS - 1) % BLOCKS
+    halo_up_last, halo_down_last = ext.at[0, pl.ds(PTS, REACH)], ext.at[0, pl.ds(REACH, REACH)]
+    to_relay = [
+        pair(halo_up_last, passing, relay_in, (next_block * GROUP + RELAY[0], g)),
+        pair(halo_down_last, passing, relay_in, (last_block * GROUP + RELAY[1], g)),
+    ]
+    relayed = [
+        pair(passing, ext.at[0, pl.ds(0, REACH)], relay_out, (block * GROUP, g)),
+        pair(passing, ext.at[0, pl.ds(REACH + PTS, REACH)], relay_out, (block * GROUP + GROUP - 1, g)),
+    ]
     mirror = pair(msend, mrecv, mir_sem, (across, g))
     sums = []
     for k in range(GROUP):
@@ -271,6 +282,20 @@
 
     lax.fori_loop(0, TILES, azimuth, 0)
 
+    def local_sums(t, carry):
+        rho = pow_t[t, 1]
+        for c in range(3):
+            ahead = back = None
+            for row in range(PTS):
+                right = ext[c, REACH + row, :, cols(t)] - STEP_WEIGHT * part[c, row, :, cols(t)]
+                ahead = right if row == 0 else rho * ahead + right
+                back = right if row == 0 else back + pow_t[t, row] * right
+            fb[t, c] = ahead
+            fb[TILES + t, c] = back
+        return carry
+
+    lax.fori_loop(0, TILES, local_sums, 0)
+
     planes_e.wait_recv()
 
     def partner_sums(t, carry):
@@ -348,42 +373,13 @@
 
     @pl.when(final)
     def _():
-        halo_up[0].start()
+        to_relay[0].start()
         halo_up[2].start()
 
     @pl.when(first)
     def _():
-        halo_down[0].start()
+        to_relay[1].start()
         halo_down[2].start()
-
-    mirror.wait_recv()
-
-    def across_axis(i, carry):
-        lines = []
-        for c in range(3):
-            packed = mrecv[c, i]
-            lines += [packed[:, :RT]] + [pltpu.roll(packed, LANES - RT * j, 1)[:, :RT] for j in range(1, 4)]
-        more = dot3(jnp.concatenate(lines, axis=0), wh[pl.ds(NR, RT)], wl[pl.ds(NR, RT)]).reshape(3, 4, 8, NR)
-        rows = pl.ds(4 * i, 4)
-        for c in range(3):
-            part[c, rows] = part[c, rows] + ext[0, pl.ds(REACH + 4 * i, 4)] * more[c]
-        return carry
-
-    lax.fori_loop(0, PTS // 4, across_axis, 0)
-
-    def local_sums(t, carry):
-        rho = pow_t[t, 1]
-        for c in range(3):
-            ahead = back = None
-            for row in range(PTS):
-                right = ext[c, REACH + row, :, cols(t)] - STEP_WEIGHT * part[c, row, :, cols(t)]
-                ahead = right if row == 0 else rho * ahead + right
-                back = right if row == 0 else back + pow_t[t, row] * right
-            fb[t, c] = ahead
-            fb[TILES + t, c] = back
-        return carry
-
-    lax.fori_loop(0, TILES, local_sums, 0)
 
     def add_halo(side, summed):
         def body(t, carry):
@@ -417,6 +413,27 @@
         for cp in (halo_down[1], halo_down[0], halo_down[2]):
             cp.wait_recv()
         add_halo(1, True)
+
+    mirror.wait_recv()
+    for i in range(PTS // 4):
+        lines = []
+        for c in range(3):
+            packed = mrecv[c, i]
+            lines += [packed[:, :RT]] + [pltpu.roll(packed, LANES - RT * j, 1)[:, :RT] for j in range(1, 4)]
+        more = dot3(jnp.concatenate(lines, axis=0), wh[pl.ds(NR, RT)], wl[pl.ds(NR, RT)]).reshape(3, 4, 8, NR)
+        for t in range(TILES):
+            here = slice(t * LANES, (t + 1) * LANES)
+            for c in range(3):
+                ahead, back = fb[t, c], fb[TILES + t, c]
+                for j in range(4):
+                    row = 4 * i + j
+                    x = ext[0, REACH + row, :, here] * more[c, j, :, here]
+                    part[c, row, :, here] = part[c, row, :, here] + x
+                    x = -STEP_WEIGHT * x
+                    ahead = ahead + pow_t[t, PTS - 1 - row] * x
+                    back = back + pow_t[t, row] * x
+                fb[t, c] = ahead
+                fb[TILES + t, c] = back
 
     one, two, three = [], [], []
     for k in sorted(range(1, GROUP), key=lambda k: abs(k - GROUP // 2)):
@@ -460,11 +477,6 @@
 
         lax.fori_loop(0, TILES, body, 0)
 
-    def write(src, dst, k):
-        cp = pltpu.make_async_copy(src, dst, out_sem.at[k])
-        cp.start()
-        return cp
-
     def entry(k):
         return k + backward * (GROUP - 1 - 2 * k)
 
@@ -491,20 +503,13 @@
         cp.start()
         two.append(cp)
 
-    @pl.when(first)
-    def _():
-        halo_up[0].wait_recv()
-        halo_up[2].wait_recv()
-        add_halo(0, False)
-
-    @pl.when(final)
-    def _():
-        halo_down[0].wait_recv()
-        halo_down[2].wait_recv()
-        add_halo(1, False)
-
-    finish_term(2)
-    writes = [write(part.at[2], non_hbm.at[2], 0)]
+
+    for side in range(2):
+
+        @pl.when(me == RELAY[side])
+        def _(side=side):
+            to_relay[side].wait_recv()
+            relayed[side].start()
 
     for cp in two:
         cp.wait_recv()
@@ -523,50 +528,71 @@
         three.append(cp)
     car[me] = ret[me]
 
+    @pl.when(first)
+    def _():
+        relayed[0].wait_recv()
+        halo_up[2].wait_recv()
+        add_halo(0, False)
+
+    @pl.when(final)
+    def _():
+        relayed[1].wait_recv()
+        halo_down[2].wait_recv()
+        add_halo(1, False)
+
+    finish_term(2)
     for c in range(2):
         planes[c].wait_recv()
         finish_term(c)
-        writes.append(write(part.at[c], non_hbm.at[c], 1 + c))
 
     for cp in three:
         cp.wait_recv()
 
-    def last(t, carry):
-        scale = scale_t[t]
-        for c in range(3):
-            from_left = scale * car[t, c]
-            from_right = scale * car[TILES + t, c]
-            for row in range(PTS):
-                loc[c, row, :, cols(t)] = (
-                    scale * loc[c, row, :, cols(t)]
-                    + pow_t[t, row + 1] * from_left
-                    + pow_t[t, PTS - row] * from_right
-                )
-        return carry
-
-    lax.fori_loop(0, TILES, last, 0)
-    writes.append(write(loc, new_hbm, 3))
-    for cp in (planes_e, *halo_up, *halo_down, mirror, *sums, *planes, *one, *two, *three):
+    for t in range(TILES):
+        ends[t] = scale_t[t] * car[t]
+        ends[TILES + t] = scale_t[t] * car[TILES + t]
+    for cp in (planes_e, *halo_up[1:], *halo_down[1:], mirror, *sums, *planes, *one, *two, *three):
         cp.wait_send()
+
+    @pl.when(me != GROUP - 1)
+    def _():
+        halo_up[0].wait_send()
+
+    @pl.when(me != 0)
+    def _():
+        halo_down[0].wait_send()
+
+    for side in range(2):
+
+        @pl.when(me == RELAY[side])
+        def _(side=side):
+            relayed[side].wait_send()
 
     for side, here in ((0, final), (1, first)):
 
         @pl.when(here)
         def _(side=side):
-            for cp in edge[side]:
+            for cp in (*edge[side], to_relay[side]):
                 cp.wait_send()
 
-    for cp in writes:
-        cp.wait()
-
-
-def write_out(new_in, non_in, new_out, non_out, sem):
-    copies = []
-    for k, (src, dst) in enumerate(((new_in, new_out), (non_in, non_out))):
-        for c in range(3):
-            copies.append(pltpu.make_async_copy(src.at[c], dst.at[c], sem.at[k, c]))
-    for cp in copies:
+
+def write_out(loc, part, ends, pow_t, scale_t, new_out, non_out, new, sem):
+    def copy(src, dst, k, c):
+        cp = pltpu.make_async_copy(src.at[c], dst.at[c], sem.at[k, c])
         cp.start()
+        return cp
+
+    copies = [copy(part, non_out, 1, c) for c in range(3)]
+    for c in range(3):
+        for t in range(TILES):
+            here = slice(t * LANES, (t + 1) * LANES)
+            for row in range(PTS):
+                new[c, row, :, here] = (
+                    scale_t[t] * loc[c, row, :, here]
+                    + pow_t[t, row + 1] * ends[t, c]
+                    + pow_t[t, PTS - row] * ends[TILES + t, c]
+                )
+        copies.append(copy(new, new_out, 0, c))
     for cp in copies:
         cp.wait()
 
@@ -579,13 +605,16 @@
         pltpu.with_memory_space_constraint(x, pltpu.HBM) for x in (velocity, radial_op.T, azimuth_stencil)
     ]
     tile = (8, LANES)
-    shapes = (jax.ShapeDtypeStruct(block, F32), jax.ShapeDtypeStruct(block, F32))
+    kept = tuple(
+        jax.ShapeDtypeStruct(shape, F32)
+        for shape in (block, block, (GROUP, 3, *tile), (TILES, PTS + 1, *tile), (TILES, *tile))
+    )
     outs = pl.pallas_call(
         kernel,
         name="substep",
-        out_shape=shapes,
+        out_shape=kept,
         in_specs=[any_space] * 3 + [pl.BlockSpec(memory_space=pltpu.SMEM)],
-        out_specs=(any_space, any_space),
+        out_specs=(pl.BlockSpec(memory_space=pltpu.VMEM),) * len(kept),
         scratch_shapes=[
             pltpu.SMEM((2 * REACH + 1,), F32),
             pltpu.VMEM((3, PTS + 2 * REACH, 8, NR), F32),
@@ -600,10 +629,6 @@
             pltpu.VMEM((3, 4, *tile), F32),
             pltpu.VMEM(block, F32),
             pltpu.VMEM(block, F32),
-            pltpu.VMEM(block, F32),
-            pltpu.VMEM(block, F32),
-            pltpu.VMEM((TILES, *tile), F32),
-            pltpu.VMEM((TILES, PTS + 1, *tile), F32),
             pltpu.VMEM((TILES, *tile), F32),
             pltpu.VMEM((TILES, *tile), F32),
             pltpu.VMEM((TILES, *tile), F32),
@@ -623,7 +648,8 @@
             dma((GROUP - 1,)), dma((GROUP - 1,)),
             dma((BLOCKS - 1,)), dma((BLOCKS - 1,)),
             dma((GROUP - 1,)), dma((GROUP - 1,)),
-            dma((4,)),
+            dma((2,)), dma((2,)),
+            pltpu.VMEM((REACH, 8, NR), F32),
             pltpu.SemaphoreType.REGULAR((3,)),
         ],
         compiler_params=pltpu.CompilerParams(
@@ -634,9 +660,9 @@
         write_out,
         name="write_out",
         out_shape=(pltpu.HBM(block, F32), pltpu.HBM(block, F32)),
-        in_specs=[pl.BlockSpec(memory_space=pltpu.VMEM)] * 2,
+        in_specs=[pl.BlockSpec(memory_space=pltpu.VMEM)] * len(kept),
         out_specs=(any_space, any_space),
-        scratch_shapes=[dma((2, 3))],
+        scratch_shapes=[pltpu.VMEM(block, F32), dma((2, 3))],
     )(*[pltpu.with_memory_space_constraint(x, pltpu.VMEM) for x in outs])
 
 

time: 42 us -> 40.4 us (0.962)
  Pallas kernels: 40.6 us -> 39 us
    pallas_call x1, Pallas kernels: 39.4 us -> 37.8 us  [local(): pl.pallas_call(kernel, name='substep', out_shape=kept, in_specs=[any_spac...]
where the time goes in v5:
time: 40.4 us; the launch traced here: 40.3 us
  Pallas kernels  39 us (97%)
  between operations  1.28 us (3%)
    pallas_call x1, Pallas kernels, local(): pl.pallas_call(kernel, name='substep', out_shape=kept, in_specs=[any_spac...  37.8 us
    pallas_call x1, Pallas kernels, local(): pl.pallas_call(write_out, name='write_out', out_shape=(pltpu.HBM(block, F...  1.19 us

profile of v5, /device:TPU:1, one launch (start us, length us, event | category | flops | bytes accessed | tf_op | source)
XLA Modules:
  0.0 40.3 jit_solution(4799535132856453953)
XLA Ops:
  1.3 37.8 %substep.1 = (f32[3,16,8,512]{3,2,1,0:T(8,128)S(1)}, f32[3,16,8,512]{3,2,1,0:T(8,128)S(1)}, f32[8,3,8,128]{3,2,1,0:T(8,128)S(1)}, f32[4,17,8,128]{3,2,1,0:T(8,128)S(1)}, f32[4,8,128]{2,1,0:T(8,128)S(1)}) custom-call(f32[3,16,8,512]{3,2,1,0:T(8,128)} %v_hbm.1, f32[544,512]{1,0:T(8,128)} %bitcast.1, f32[21]{0:T(128)} %sten_hbm.1, f32[1]{0:T(128)S(6)} %copy.6.visc), custom_call_target="tpu_custom_call" | custom-call | tf_op jit(solution)/shard_map/substep/pallas_call | solution.py:612
  39.1 1.2 %write_out.1 = (f32[3,16,8,512]{3,2,1,0:T(8,128)}, f32[3,16,8,512]{3,2,1,0:T(8,128)}) custom-call(f32[3,16,8,512]{3,2,1,0:T(8,128)S(1)} %get-tuple-element.7.loc, f32[3,16,8,512]{3,2,1,0:T(8,128)S(1)} %get-tuple-element.8.part, f32[8,3,8,128]{3,2,1,0:T(8,128)S(1)} %get-tuple-element.9.ends, f32[4,17,8,128]{3,2,1,0:T(8,128)S(1)} %get-tuple-element.10.pow_t, ...), custom_call_target="tpu_custom_call" | custom-call | tf_op jit(solution)/shard_map/write_out/pallas_call | solution.py:659

commit v6 on v5

--- a/solution.py
+++ b/solution.py
@@ -180,12 +180,6 @@
         pair(passing, ext.at[0, pl.ds(REACH + PTS, REACH)], relay_out, (block * GROUP + GROUP - 1, g)),
     ]
     mirror = pair(msend, mrecv, mir_sem, (across, g))
-    sums = []
-    for k in range(GROUP):
-        other = (me + k) % GROUP
-        sums.append(
-            remote(ssend.at[other], sum_in.at[me], v_s.at[k], v_r.at[k], (block * GROUP + other, 1 - g))
-        )
     planes = [
         remote(gsend.at[c], grecv.at[c], g_sem.at[0, c], g_sem.at[1, c], (p, 1 - g)) for c in range(2)
     ]
@@ -296,9 +290,21 @@
 
     lax.fori_loop(0, TILES, local_sums, 0)
 
+    @pl.when(final)
+    def _():
+        halo_down[1].wait_recv()
+        to_relay[0].start()
+
+    @pl.when(first)
+    def _():
+        halo_up[1].wait_recv()
+        to_relay[1].start()
+
     planes_e.wait_recv()
 
-    def partner_sums(t, carry):
+    sums = []
+    for turn in range(TILES):
+        t = (my_tile + turn) % TILES
         rho = pow_t[t, 1]
         e = []
         for i in range(PTS // 4):
@@ -311,11 +317,12 @@
                 back = x if row == 0 else back + pow_t[t, row] * x
             ssend[t, c] = -STEP_WEIGHT * ahead
             ssend[TILES + t, c] = -STEP_WEIGHT * back
-        return carry
-
-    lax.fori_loop(0, TILES, partner_sums, 0)
-    for cp in sums:
-        cp.start()
+        for k in (t, TILES + t):
+            cp = remote(
+                ssend.at[k], sum_in.at[me], v_s.at[len(sums)], v_r.at[0], (block * GROUP + k, 1 - g)
+            )
+            cp.start()
+            sums.append(cp)
 
     def halo_taps(t, c, row, shift):
         span = range(row, REACH) if shift[0] == 0 else range(REACH + PTS, row + 2 * REACH + 1)
@@ -356,14 +363,12 @@
 
     @pl.when(final)
     def _():
-        halo_down[1].wait_recv()
         edge_sums(0)
         for cp in edge[0]:
             cp.start()
 
     @pl.when(first)
     def _():
-        halo_up[1].wait_recv()
         edge_sums(1)
         for cp in edge[1]:
             cp.start()
@@ -373,12 +378,10 @@
 
     @pl.when(final)
     def _():
-        to_relay[0].start()
         halo_up[2].start()
 
     @pl.when(first)
     def _():
-        to_relay[1].start()
         halo_down[2].start()
 
     def add_halo(side, summed):
@@ -481,8 +484,9 @@
         return k + backward * (GROUP - 1 - 2 * k)
 
     pl.semaphore_wait(chain.at[2], 1)
-    for cp in (*one, *sums, edge[0][0], edge[1][0]):
+    for cp in (*one, edge[0][0], edge[1][0]):
         cp.wait_recv()
+    remote(ssend, sum_in, v_s.at[0], v_r.at[0], (p, 1 - g)).wait_recv()
     for k in range(GROUP):
         total = up_in[k] + sum_in[k]
         if k == 0:
@@ -644,7 +648,7 @@
             pltpu.VMEM((GROUP, 3, *tile), F32),
             dma((4,)),
             dma((2,)), dma((2,)), dma((2, 3)), dma((2, 3)),
-            dma((2, 2)), dma((GROUP,)), dma((GROUP,)), dma((GROUP,)), dma((2,)),
+            dma((2, 2)), dma((GROUP,)), dma((1,)), dma((GROUP,)), dma((2,)),
             dma((GROUP - 1,)), dma((GROUP - 1,)),
             dma((BLOCKS - 1,)), dma((BLOCKS - 1,)),
             dma((GROUP - 1,)), dma((GROUP - 1,)),

time: 40.4 us -> 39.6 us (0.980)
  Pallas kernels: 39 us -> 38.2 us
    pallas_call x1, Pallas kernels: 37.8 us -> 37 us  [local(): pl.pallas_call(kernel, name='substep', out_shape=kept, in_specs=[any_spac...]
where the time goes in v6:
time: 39.6 us; the launch traced here: 39.5 us
  Pallas kernels  38.2 us (96%)
  between operations  1.28 us (3%)
    pallas_call x1, Pallas kernels, local(): pl.pallas_call(kernel, name='substep', out_shape=kept, in_specs=[any_spac...  37 us
    pallas_call x1, Pallas kernels, local(): pl.pallas_call(write_out, name='write_out', out_shape=(pltpu.HBM(block, F...  1.19 us

profile of v6, /device:TPU:1, one launch (start us, length us, event | category | flops | bytes accessed | tf_op | source)
XLA Modules:
  0.0 39.5 jit_solution(1377295434427120110)
XLA Ops:
  1.3 37.0 %substep.1 = (f32[3,16,8,512]{3,2,1,0:T(8,128)S(1)}, f32[3,16,8,512]{3,2,1,0:T(8,128)S(1)}, f32[8,3,8,128]{3,2,1,0:T(8,128)S(1)}, f32[4,17,8,128]{3,2,1,0:T(8,128)S(1)}, f32[4,8,128]{2,1,0:T(8,128)S(1)}) custom-call(f32[3,16,8,512]{3,2,1,0:T(8,128)} %v_hbm.1, f32[544,512]{1,0:T(8,128)} %bitcast.1, f32[21]{0:T(128)} %sten_hbm.1, f32[1]{0:T(128)S(6)} %copy.6.visc), custom_call_target="tpu_custom_call" | custom-call | tf_op jit(solution)/shard_map/substep/pallas_call | solution.py:616
  38.3 1.2 %write_out.1 = (f32[3,16,8,512]{3,2,1,0:T(8,128)}, f32[3,16,8,512]{3,2,1,0:T(8,128)}) custom-call(f32[3,16,8,512]{3,2,1,0:T(8,128)S(1)} %get-tuple-element.7.loc, f32[3,16,8,512]{3,2,1,0:T(8,128)S(1)} %get-tuple-element.8.part, f32[8,3,8,128]{3,2,1,0:T(8,128)S(1)} %get-tuple-element.9.ends, f32[4,17,8,128]{3,2,1,0:T(8,128)S(1)} %get-tuple-element.10.pow_t, ...), custom_call_target="tpu_custom_call" | custom-call | tf_op jit(solution)/shard_map/write_out/pallas_call | solution.py:663

commit v7 on v6

--- a/solution.py
+++ b/solution.py
@@ -221,6 +221,9 @@
             pow_t[t, j] = power
             power = power * rho[:, here]
 
+    pl.semaphore_wait(chain.at[0], 2)
+    tell(1, hop[2:])
+
     def spread(t, carry):
         for c in range(3):
             for i in range(PTS // 4):
@@ -237,9 +240,6 @@
         return carry
 
     lax.fori_loop(0, TILES, spread, 0)
-
-    pl.semaphore_wait(chain.at[0], 2)
-    tell(1, hop[2:])
 
     reads[1].wait()
     op_high, op_low = split(op_v[...])
@@ -294,11 +294,13 @@
     def _():
         halo_down[1].wait_recv()
         to_relay[0].start()
+        halo_up[2].start()
 
     @pl.when(first)
     def _():
         halo_up[1].wait_recv()
         to_relay[1].start()
+        halo_down[2].start()
 
     planes_e.wait_recv()
 
@@ -375,14 +377,6 @@
 
     for cp in planes:
         cp.start()
-
-    @pl.when(final)
-    def _():
-        halo_up[2].start()
-
-    @pl.when(first)
-    def _():
-        halo_down[2].start()
 
     def add_halo(side, summed):
         def body(t, carry):

time: 39.6 us -> 38.9 us (0.982)
  Pallas kernels: 38.2 us -> 37.5 us
    pallas_call x1, Pallas kernels: 37 us -> 36.4 us  [local(): pl.pallas_call(kernel, name='substep', out_shape=kept, in_specs=[any_spac...]
where the time goes in v7:
time: 38.9 us; the launch traced here: 38.8 us
  Pallas kernels  37.5 us (96%)
  between operations  1.28 us (3%)
    pallas_call x1, Pallas kernels, local(): pl.pallas_call(kernel, name='substep', out_shape=kept, in_specs=[any_spac...  36.4 us
    pallas_call x1, Pallas kernels, local(): pl.pallas_call(write_out, name='write_out', out_shape=(pltpu.HBM(block, F...  1.19 us

profile of v7, /device:TPU:1, one launch (start us, length us, event | category | flops | bytes accessed | tf_op | source)
XLA Modules:
  0.0 38.8 jit_solution(3970755598049010545)
XLA Ops:
  1.3 36.4 %substep.1 = (f32[3,16,8,512]{3,2,1,0:T(8,128)S(1)}, f32[3,16,8,512]{3,2,1,0:T(8,128)S(1)}, f32[8,3,8,128]{3,2,1,0:T(8,128)S(1)}, f32[4,17,8,128]{3,2,1,0:T(8,128)S(1)}, f32[4,8,128]{2,1,0:T(8,128)S(1)}) custom-call(f32[3,16,8,512]{3,2,1,0:T(8,128)} %v_hbm.1, f32[544,512]{1,0:T(8,128)} %bitcast.1, f32[21]{0:T(128)} %sten_hbm.1, f32[1]{0:T(128)S(6)} %copy.6.visc), custom_call_target="tpu_custom_call" | custom-call | tf_op jit(solution)/shard_map/substep/pallas_call | solution.py:610
  37.6 1.2 %write_out.1 = (f32[3,16,8,512]{3,2,1,0:T(8,128)}, f32[3,16,8,512]{3,2,1,0:T(8,128)}) custom-call(f32[3,16,8,512]{3,2,1,0:T(8,128)S(1)} %get-tuple-element.7.loc, f32[3,16,8,512]{3,2,1,0:T(8,128)S(1)} %get-tuple-element.8.part, f32[8,3,8,128]{3,2,1,0:T(8,128)S(1)} %get-tuple-element.9.ends, f32[4,17,8,128]{3,2,1,0:T(8,128)S(1)} %get-tuple-element.10.pow_t, ...), custom_call_target="tpu_custom_call" | custom-call | tf_op jit(solution)/shard_map/write_out/pallas_call | solution.py:657

commit v8 on v7

--- a/solution.py
+++ b/solution.py
@@ -375,8 +375,7 @@
         for cp in edge[1]:
             cp.start()
 
-    for cp in planes:
-        cp.start()
+    planes[0].start()
 
     def add_halo(side, summed):
         def body(t, carry):
@@ -500,6 +499,7 @@
         )
         cp.start()
         two.append(cp)
+    planes[1].start()
 
 
     for side in range(2):

time: 38.9 us -> 38.9 us (level)
  no operation moved by 1% of the time
where the time goes in v8:
time: 38.9 us; the launch traced here: 38.8 us
  Pallas kernels  37.5 us (96%)
  between operations  1.28 us (3%)
    pallas_call x1, Pallas kernels, local(): pl.pallas_call(kernel, name='substep', out_shape=kept, in_specs=[any_spac...  36.3 us
    pallas_call x1, Pallas kernels, local(): pl.pallas_call(write_out, name='write_out', out_shape=(pltpu.HBM(block, F...  1.19 us

profile of v8, /device:TPU:1, one launch (start us, length us, event | category | flops | bytes accessed | tf_op | source)
XLA Modules:
  0.0 38.8 jit_solution(7284924753027106732)
XLA Ops:
  1.3 36.3 %substep.1 = (f32[3,16,8,512]{3,2,1,0:T(8,128)S(1)}, f32[3,16,8,512]{3,2,1,0:T(8,128)S(1)}, f32[8,3,8,128]{3,2,1,0:T(8,128)S(1)}, f32[4,17,8,128]{3,2,1,0:T(8,128)S(1)}, f32[4,8,128]{2,1,0:T(8,128)S(1)}) custom-call(f32[3,16,8,512]{3,2,1,0:T(8,128)} %v_hbm.1, f32[544,512]{1,0:T(8,128)} %bitcast.1, f32[21]{0:T(128)} %sten_hbm.1, f32[1]{0:T(128)S(6)} %copy.6.visc), custom_call_target="tpu_custom_call" | custom-call | tf_op jit(solution)/shard_map/substep/pallas_call | solution.py:610
  37.6 1.2 %write_out.1 = (f32[3,16,8,512]{3,2,1,0:T(8,128)}, f32[3,16,8,512]{3,2,1,0:T(8,128)}) custom-call(f32[3,16,8,512]{3,2,1,0:T(8,128)S(1)} %get-tuple-element.7.loc, f32[3,16,8,512]{3,2,1,0:T(8,128)S(1)} %get-tuple-element.8.part, f32[8,3,8,128]{3,2,1,0:T(8,128)S(1)} %get-tuple-element.9.ends, f32[4,17,8,128]{3,2,1,0:T(8,128)S(1)} %get-tuple-element.10.pow_t, ...), custom_call_target="tpu_custom_call" | custom-call | tf_op jit(solution)/shard_map/write_out/pallas_call | solution.py:657

commit v9 on v8

--- a/solution.py
+++ b/solution.py
@@ -375,8 +375,6 @@
         for cp in edge[1]:
             cp.start()
 
-    planes[0].start()
-
     def add_halo(side, summed):
         def body(t, carry):
             inv, rho = inv_t[t], pow_t[t, 1]
@@ -438,6 +436,7 @@
         cp.start()
         one.append(cp)
     up_in[me] = fb[me]
+    planes[0].start()
 
     def finish_term(c):
         def body(t, carry):

time: 38.9 us -> 38.8 us (level)
  no operation moved by 1% of the time
where the time goes in v9:
time: 38.8 us; the launch traced here: 38.7 us
  Pallas kernels  37.4 us (96%)
  between operations  1.28 us (3%)
    pallas_call x1, Pallas kernels, local(): pl.pallas_call(kernel, name='substep', out_shape=kept, in_specs=[any_spac...  36.2 us
    pallas_call x1, Pallas kernels, local(): pl.pallas_call(write_out, name='write_out', out_shape=(pltpu.HBM(block, F...  1.19 us

profile of v9, /device:TPU:1, one launch (start us, length us, event | category | flops | bytes accessed | tf_op | source)
XLA Modules:
  0.0 38.7 jit_solution(7695526460400740621)
XLA Ops:
  1.3 36.2 %substep.1 = (f32[3,16,8,512]{3,2,1,0:T(8,128)S(1)}, f32[3,16,8,512]{3,2,1,0:T(8,128)S(1)}, f32[8,3,8,128]{3,2,1,0:T(8,128)S(1)}, f32[4,17,8,128]{3,2,1,0:T(8,128)S(1)}, f32[4,8,128]{2,1,0:T(8,128)S(1)}) custom-call(f32[3,16,8,512]{3,2,1,0:T(8,128)} %v_hbm.1, f32[544,512]{1,0:T(8,128)} %bitcast.1, f32[21]{0:T(128)} %sten_hbm.1, f32[1]{0:T(128)S(6)} %copy.6.visc), custom_call_target="tpu_custom_call" | custom-call | tf_op jit(solution)/shard_map/substep/pallas_call | solution.py:609
  37.5 1.2 %write_out.1 = (f32[3,16,8,512]{3,2,1,0:T(8,128)}, f32[3,16,8,512]{3,2,1,0:T(8,128)}) custom-call(f32[3,16,8,512]{3,2,1,0:T(8,128)S(1)} %get-tuple-element.7.loc, f32[3,16,8,512]{3,2,1,0:T(8,128)S(1)} %get-tuple-element.8.part, f32[8,3,8,128]{3,2,1,0:T(8,128)S(1)} %get-tuple-element.9.ends, f32[4,17,8,128]{3,2,1,0:T(8,128)S(1)} %get-tuple-element.10.pow_t, ...), custom_call_target="tpu_custom_call" | custom-call | tf_op jit(solution)/shard_map/write_out/pallas_call | solution.py:656
